TPU v7x, 256 devices: a whole 4x4x8 slice. The times are simulated.
256 devices in a mesh: expert: 64 (over y, z, core), etp: 4 (over x).
Axes of the slice: x: 4, y: 4, z: 8, core: 2. Of those that a mesh axis runs over, the one named last changes fastest.
Arguments:
- tokens: bfloat16 [8192, 2048], P('expert'), may hold values from -6 to 6
- grad_out: bfloat16 [8192, 2048], P('expert'), may hold values from -6 to 6
- routes: int32 [8192, 8], P('expert'), may hold values from 0 to 127, all different within a row; in each aligned block of 128 rows (0 to 127, 128 to 255, ...) at most 10 rows name the same one
- probs: bfloat16 [8192, 8], P('expert'), may hold values from 0.049804688 to 0.3984375
- w_gate: bfloat16 [128, 768, 2048], P('expert', 'etp'), may hold values from -0.125 to 0.125
- w_up: bfloat16 [128, 768, 2048], P('expert', 'etp'), may hold values from -0.125 to 0.125
- w_down: bfloat16 [128, 768, 2048], P('expert', 'etp'), may hold values from -0.21875 to 0.21875
Outputs:
- grad_tokens: bfloat16 [8192, 2048], P('expert')
- grad_probs: bfloat16 [8192, 8], P('expert')
- grad_gate: bfloat16 [128, 768, 2048], P('expert', 'etp')
- grad_up: bfloat16 [128, 768, 2048], P('expert', 'etp')
- grad_down: bfloat16 [128, 768, 2048], P('expert', 'etp')
Inputs may be any that keep to these rules, and one draw needn't show every extreme that they name: `routes`: each row names 8 different experts. Among the 128 rows of one device no expert is named by more than 10 rows, a bound that some block reaches.
All inputs are finite; a program needn't handle non-finite values.
Results may differ from a plain program's by a relative error of at most 0.018.
Values may be sent and summed in bfloat16 or wider, within the bound.
A program may use at most 128 MiB of HBM per device.

v0:
```python
import functools

import jax
import jax.numpy as jnp
from jax import lax
from jax.experimental import pallas as pl
from jax.experimental.pallas import tpu as pltpu
from jax.sharding import Mesh, PartitionSpec as P

NY, NZ, NC, NX = 4, 8, 2, 4
SLOTS = 10
LE = 2
TOK = 128
GROUP = 4 * NC * SLOTS
LANES = 512
BF = jnp.bfloat16
F32 = jnp.float32
MESH = pl.DeviceIdType.MESH
PLACE = {0: 0, 1: 1, 7: 2, 2: 3, 6: 4, 3: 5, 5: 6, 4: 7}


def remote(src, dst, send, recv, **where):
    return pltpu.make_async_remote_copy(
        src_ref=src, dst_ref=dst, send_sem=send, recv_sem=recv, device_id=where, device_id_type=MESH
    )


def axes():
    return tuple(lax.axis_index(n) for n in ("y", "z", "c", "x"))


def dispatch_kernel(
    mine, info, rows, pick_out,
    blocks, infos, pick_w, out_y, relay,
    i_send, i_recv, z_send, z_recv, p_send, p_recv, y_send, y_recv, r_send, r_recv, x_send, x_recv, l_sem, s_sem,
):
    y, z, c, x = axes()
    h = x % 2
    other = 1 - c
    sign = 1 - 2 * c
    z_long, z_short = (z + sign + NZ) % NZ, (z - sign + NZ) % NZ
    y_up, y_down = (y + 1) % NY, (y + NY - 1) % NY
    x_up, x_down = (x + 1) % NX, (x + NX - 1) % NX

    barrier = pltpu.get_barrier_semaphore()
    for m in range(NZ):
        for cc in ((c, other) if m else (other,)):
            pl.semaphore_signal(barrier, inc=1, device_id={"z": (z + m) % NZ, "c": cc}, device_id_type=MESH)
    for yy in (y_up, y_down):
        pl.semaphore_signal(barrier, inc=1, device_id={"y": yy}, device_id_type=MESH)
    for xx in (x_up, x_down):
        pl.semaphore_signal(barrier, inc=1, device_id={"x": xx}, device_id_type=MESH)
    pl.semaphore_wait(barrier, 2 * NZ - 1 + 4)

    waits = []

    def go(copy):
        copy.start()
        waits.append(copy)

    def info_copy(m, cc, far):
        at = PLACE[(NZ - m) % NZ]
        return remote(
            info, infos.at[at, c], i_send.at[m, far], i_recv.at[at, c], z=(z + m) % NZ, c=cc
        )

    for m in range(NZ):
        if m:
            go(info_copy(m, c, 0))
        go(info_copy(m, other, 1))

    def place(long, s):
        if s == 0:
            return 0
        if long:
            return 7 if s == 4 else 2 * s - c
        return 2 * s - 1 + c

    def hop(k, long, s):
        index = (s - 1) if long else (3 + s)
        src = mine.at[k] if s == 1 else blocks.at[k, place(long, s - 1), c]
        return remote(
            src, blocks.at[k, place(long, s), c], z_send.at[k, index], z_recv.at[k, index],
            z=z_long if long else z_short,
        )

    def to_partner(k, at):
        src = mine.at[k] if isinstance(at, int) and at == 0 else blocks.at[k, at, c]
        return remote(src, blocks.at[k, at, c], p_send.at[k, at], p_recv.at[k, at], c=other)

    def start_chunk(k):
        go(hop(k, True, 1))
        go(hop(k, False, 1))
        go(to_partner(k, 0))
        keep = pltpu.make_async_copy(mine.at[k], blocks.at[k, 0, c], l_sem.at[k])
        keep.start()
        return keep

    keeps = {0: start_chunk(0)}

    def z_step(k, s):
        for long in ((True, False) if s < 4 else (True,)):
            hop(k, long, s).wait_recv()
            if s < (4 if long else 3):
                go(hop(k, long, s + 1))
            go(to_partner(k, place(long, s)))

    def y_piece(k, g, d, le):
        src = out_y.at[k, g, d, le]
        slot = 4 * (k // 2) + 2 * h + k % 2
        landing = rows.at[slot, le, y, g]
        sems = dict(send=y_send.at[k, g, d - 1, le], recv=y_recv.at[k, g, d - 1, le])
        if d == 1:
            return remote(src, landing, y=y_up, **sems)
        if d == 3:
            return remote(src, landing, y=y_down, **sems)
        return remote(src, relay.at[k, g, le], y=y_up if le == 0 else y_down, **sems)

    def relayed(k, g, le):
        slot = 4 * (k // 2) + 2 * h + k % 2
        came = y_down if le == 0 else y_up
        return remote(
            relay.at[k, g, le], rows.at[slot, le, came, g], r_send.at[k, g, le], r_recv.at[k, g, le],
            y=y_up if le == 0 else y_down,
        )

    def x_piece(k, g, d, le):
        slot = 4 * (k // 2) + 2 * h + k % 2
        there = rows.at[slot, le, (y + NY - d) % NY, g]
        src = out_y.at[k, g, 0, le] if d == 0 else there
        return remote(
            src, there, x_send.at[k, g, d, le], x_recv.at[k, g, d, le], x=x_up if le == 0 else x_down
        )

    def own_piece(k, g, le):
        slot = 4 * (k // 2) + 2 * h + k % 2
        return pltpu.make_async_copy(
            out_y.at[k, g, 0, le], rows.at[slot, le, y, g], s_sem.at[k, g, le]
        )

    def pick_rows(k, g):
        if k in keeps:
            keeps.pop(k).wait()
        for at in range(4 * g, 4 * g + 4):
            remote(
                mine.at[k], blocks.at[k, at, other], p_send.at[k, at], p_recv.at[k, at], c=other
            ).wait_recv()
        chosen = pick_out[g] if k < 2 else pick_w[g]
        got = jnp.dot(
            chosen,
            blocks[k, 4 * g : 4 * g + 4].reshape(4 * NC * TOK, LANES),
            preferred_element_type=F32,
        ).astype(BF)
        out_y[k, g] = got.reshape(NY, LE, GROUP, LANES)
        for le in range(LE):
            go(y_piece(k, g, 2, le))
        for le in range(LE):
            go(y_piece(k, g, 1, le))
            go(y_piece(k, g, 3, le))
        for le in range(LE):
            go(x_piece(k, g, 0, le))
            own_piece(k, g, le).start()

    def y_step(k, g):
        for le in range(LE):
            y_piece(k, g, 2, le).wait_recv()
            go(relayed(k, g, le))
        for le in range(LE):
            y_piece(k, g, 1, le).wait_recv()
            go(x_piece(k, g, 1, le))
            y_piece(k, g, 3, le).wait_recv()
            go(x_piece(k, g, 3, le))

    def y_last(k, g):
        for le in range(LE):
            relayed(k, g, le).wait_recv()
            go(x_piece(k, g, 2, le))

    infos[0, c] = info[...]
    for at in range(NZ):
        if at:
            remote(info, infos.at[at, c], i_send.at[0, 0], i_recv.at[at, c], c=other).wait_recv()
        remote(info, infos.at[at, other], i_send.at[0, 0], i_recv.at[at, other], c=other).wait_recv()

    row = lax.broadcasted_iota(jnp.int32, (NY * LE, TOK), 0)
    expert = ((((y + row // LE) % NY * NZ + z) * NC + c) * LE + row % LE).astype(F32)
    before = (
        lax.broadcasted_iota(jnp.int32, (TOK, TOK), 0) < lax.broadcasted_iota(jnp.int32, (TOK, TOK), 1)
    ).astype(F32).astype(BF)
    hits, weights = [], []
    for at in range(NZ):
        for cc in range(NC):
            named = infos[at, cc].astype(F32)
            hit = jnp.zeros((NY * LE, TOK), F32)
            weight = jnp.zeros((NY * LE, TOK), F32)
            for k in range(8):
                same = named[k : k + 1] == expert
                hit = jnp.where(same, 1.0, hit)
                weight = jnp.where(same, named[8 + k : 9 + k], weight)
            hits.append(hit)
            weights.append(weight)
    ranks = jnp.dot(jnp.concatenate(hits, axis=0).astype(BF), before, preferred_element_type=F32)
    slot_row = lax.broadcasted_iota(jnp.int32, (GROUP, TOK), 0).astype(F32)
    for s in range(NZ * NC):
        g, i = s // 8, s % 8
        goal = jnp.where(
            hits[s] > 0, ranks[s * NY * LE : (s + 1) * NY * LE] + float(SLOTS * i), -1.0
        )
        for e in range(NY * LE):
            same = slot_row == goal[e : e + 1]
            at = (g, pl.ds(e * GROUP, GROUP), pl.ds(i * TOK, TOK))
            pick_out[at] = jnp.where(same, 1.0, 0.0).astype(BF)
            pick_w[at] = jnp.where(same, weights[s][e : e + 1], 0.0).astype(BF)

    for k in range(4):
        z_step(k, 1)
        if k:
            y_step(k - 1, 0)
        z_step(k, 2)
        if k < 3:
            keeps[k + 1] = start_chunk(k + 1)
        pick_rows(k, 0)
        z_step(k, 3)
        if k:
            y_last(k - 1, 0)
            y_step(k - 1, 1)
        z_step(k, 4)
        pick_rows(k, 1)
        if k:
            y_last(k - 1, 1)
    y_step(3, 0)
    y_last(3, 0)
    y_step(3, 1)
    y_last(3, 1)
    for k in range(4):
        for g in range(2):
            for le in range(LE):
                own_piece(k, g, le).wait()
                for d in range(NY):
                    slot = 4 * (k // 2) + 2 * (1 - h) + k % 2
                    there = rows.at[slot, le, (y + NY - d) % NY, g]
                    remote(
                        there, there, x_send.at[k, g, d, le], x_recv.at[k, g, d, le],
                        x=x_up if le == 0 else x_down,
                    ).wait_recv()
    for copy in waits:
        copy.wait_send()


def dispatch(mine, info):
    vmem = pl.BlockSpec(memory_space=pltpu.VMEM)
    anyw = pl.BlockSpec(memory_space=pl.ANY)
    dma = pltpu.SemaphoreType.DMA
    return pl.pallas_call(
        dispatch_kernel,
        out_shape=(
            jax.ShapeDtypeStruct((8, LE, NY, 2, GROUP, LANES), BF),
            jax.ShapeDtypeStruct((2, NY * LE * GROUP, 4 * NC * TOK), BF),
        ),
        in_specs=[vmem, vmem],
        out_specs=(anyw, vmem),
        scratch_shapes=[
            pltpu.VMEM((4, NZ, NC, TOK, LANES), BF),
            pltpu.VMEM((NZ, NC, 16, TOK), BF),
            pltpu.VMEM((2, NY * LE * GROUP, 4 * NC * TOK), BF),
            pltpu.VMEM((4, 2, NY, LE, GROUP, LANES), BF),
            pltpu.VMEM((4, 2, LE, GROUP, LANES), BF),
            dma((NZ, 2)), dma((NZ, NC)),
            dma((4, 7)), dma((4, 7)),
            dma((4, NZ)), dma((4, NZ)),
            dma((4, 2, 3, LE)), dma((4, 2, 3, LE)),
            dma((4, 2, LE)), dma((4, 2, LE)),
            dma((4, 2, NY, LE)), dma((4, 2, NY, LE)),
            dma((4,)), dma((4, 2, LE)),
        ],
        compiler_params=pltpu.CompilerParams(
            collective_id=0, has_side_effects=True, vmem_limit_bytes=48 << 20
        ),
        name="dispatch",
    )(mine, info)


def nt(a, b):
    return lax.dot_general(a, b, (((1,), (1,)), ((), ())), preferred_element_type=F32)


def tn(a, b):
    return lax.dot_general(a, b, (((0,), (0,)), ((), ())), preferred_element_type=F32)


def expert_kernel(rows, w_gate, w_up, w_down, g_gate, g_up, g_down, part, probs):
    def cut(q):
        return slice(q * LANES, (q + 1) * LANES)

    gate = sum(nt(rows[q, 0], w_gate[0, :, cut(q)]) for q in range(4))
    up = sum(nt(rows[q, 0], w_up[0, :, cut(q)]) for q in range(4))
    back = sum(nt(rows[4 + q, 0], w_down[0, :, cut(q)]) for q in range(4))
    sig = 1.0 / (1.0 + jnp.exp(-gate))
    act = gate * sig
    hidden = (act * up).astype(BF)
    d_gate = (back * up * sig * (1.0 + gate * (1.0 - sig))).astype(BF)
    d_up = (back * act).astype(BF)
    product = (hidden.astype(F32) * back).astype(BF)
    probs[0] = nt(jnp.ones((16, product.shape[1]), BF), product).astype(BF)
    for q in range(4):
        g_down[0, :, cut(q)] = tn(hidden, rows[4 + q, 0]).astype(BF)
        g_gate[0, :, cut(q)] = tn(d_gate, rows[q, 0]).astype(BF)
        g_up[0, :, cut(q)] = tn(d_up, rows[q, 0]).astype(BF)
        part[q, 0] = (
            jnp.dot(d_gate, w_gate[0, :, cut(q)], preferred_element_type=F32)
            + jnp.dot(d_up, w_up[0, :, cut(q)], preferred_element_type=F32)
        ).astype(BF)


def experts(rows, w_gate, w_up, w_down):
    le, hid, width = w_gate.shape
    n = rows.shape[2]
    weight = pl.BlockSpec((1, hid, width), lambda i: (i, 0, 0))
    return pl.pallas_call(
        expert_kernel,
        grid=(le,),
        out_shape=(
            jax.ShapeDtypeStruct((le, hid, width), BF),
            jax.ShapeDtypeStruct((le, hid, width), BF),
            jax.ShapeDtypeStruct((le, hid, width), BF),
            jax.ShapeDtypeStruct((4, le, n, LANES), BF),
            jax.ShapeDtypeStruct((le, 16, n), BF),
        ),
        in_specs=[pl.BlockSpec((8, 1, n, LANES), lambda i: (0, i, 0, 0)), weight, weight, weight],
        out_specs=(
            weight, weight, weight,
            pl.BlockSpec((4, 1, n, LANES), lambda i: (0, i, 0, 0)),
            pl.BlockSpec((1, 16, n), lambda i: (i, 0, 0)),
        ),
        compiler_params=pltpu.CompilerParams(vmem_limit_bytes=56 << 20),
        cost_estimate=pl.CostEstimate(flops=8_000_000_000, bytes_accessed=25_000_000, transcendentals=250_000),
        name="experts",
    )(rows, w_gate, w_up, w_down)


def dot(spec, a, b):
    return jnp.einsum(spec, a, b, preferred_element_type=F32)


def body(tokens, grad_out, routes, probs, w_gate, w_up, w_down):
    x = lax.axis_index("x")
    z = lax.axis_index("z")
    c = lax.axis_index("c")
    h = x % 2
    half = 2 * LANES
    quarter = LANES
    tok_rows = TOK
    le = LE
    cut = [
        lax.dynamic_slice_in_dim(a, h * half + q * LANES, LANES, axis=1)
        for a in (tokens, grad_out)
        for q in range(2)
    ]
    info = jnp.concatenate([routes.T.astype(BF), probs.T], axis=0)
    rows, pick = dispatch(jnp.stack(cut), info)
    g_gate, g_up, g_down, part, prob = experts(
        rows.reshape(8, LE, NY * 2 * GROUP, LANES), w_gate, w_up, w_down
    )
    up_ring = [(i, (i + 1) % NX) for i in range(NX)]
    down_ring = [(i, (i + NX - 1) % NX) for i in range(NX)]
    part = part.reshape(2, 2, LE, NY * 2 * GROUP, LANES)
    keep = jnp.where(h == 0, part[0], part[1])
    give = jnp.where(h == 0, part[1], part[0])
    got0 = lax.ppermute(give[:, 0], "x", up_ring)
    got1 = lax.ppermute(give[:, 1], "x", down_ring)
    kept = (keep.astype(F32) + jnp.stack([got0, got1], axis=1).astype(F32)).astype(BF)
    kept = kept.reshape(2, LE, NY, 2, GROUP, LANES)
    kept = lax.all_to_all(kept, "y", split_axis=2, concat_axis=2, tiled=True)
    y = lax.axis_index("y")
    kept = jnp.roll(kept, -y, axis=2)
    pr = prob[:, 0].reshape(LE, NY, 2, GROUP)
    pr = lax.all_to_all(pr, "y", split_axis=1, concat_axis=1, tiled=True)
    pr = jnp.roll(pr, -y, axis=1)
    pick6 = pick.reshape(2, NY, LE, GROUP, 4 * NC, TOK)
    home = dot("gyljst,qlygjd->gstqd", pick6, kept).astype(BF)
    home = home.reshape(NZ, NC, TOK, half)
    home = jnp.roll(jnp.stack([home[PLACE[r]] for r in range(NZ)]), z, axis=0).reshape(NZ * NC, TOK, half)
    home = lax.psum_scatter(home, ("z", "c"), scatter_dimension=0, tiled=False)
    ptok = dot("gyljst,lygj->gsylt", pick6, pr).astype(BF).reshape(NZ, NC, NY, LE, TOK)
    ptok = jnp.roll(jnp.roll(jnp.stack([ptok[PLACE[r]] for r in range(NZ)]), z, axis=0), y, axis=2).reshape(NZ * NC, NY * LE, TOK)
    ptok = lax.all_to_all(ptok, ("z", "c"), split_axis=0, concat_axis=0, tiled=True)
    ptok = lax.psum(ptok.astype(F32), "x")
    zeros = jnp.zeros_like(home)
    wide = jnp.where(h == 0, jnp.concatenate([home, zeros], -1), jnp.concatenate([zeros, home], -1))
    grad_tokens = lax.psum(wide, "x")
    by_expert = jnp.transpose(ptok.reshape(NZ * NC, NY, le, tok_rows), (1, 0, 2, 3)).reshape(-1, tok_rows)
    chosen = routes[:, :, None] == jnp.arange(by_expert.shape[0])[None, None, :]
    total = jnp.sum(jnp.where(chosen, by_expert.T[:, None, :], 0), axis=-1)
    grad_probs = (total / probs.astype(F32)).astype(BF)
    return (grad_tokens, grad_probs, g_gate, g_up, g_down)


def solution(mesh):
    cut = Mesh(mesh.devices.reshape(NY, NZ, NC, NX), ("y", "z", "c", "x"))
    rows = P(("y", "z", "c"), None)
    weights = P(("y", "z", "c"), "x", None)
    return jax.shard_map(
        body,
        mesh=cut,
        in_specs=(rows, rows, rows, rows, weights, weights, weights),
        out_specs=(rows, rows, weights, weights, weights),
        check_vma=False,
    )
```

profile of v0, /device:TPU:8, one launch (start us, length us, event | category | flops | bytes accessed | tf_op | source)
XLA Modules:
  0.0 360.5 jit_solution(7088667810762921776)
XLA Ops:
  8.0 0.7 convert_bitcast_fusion.1
  8.7 0.7 pad_maximum_fusion.1.info
  9.4 1.1 dynamic-slice_bitcast_fusion.1
  10.5 0.1 pad_maximum_fusion.mine
  10.6 103.9 %dispatch.1 = (bf16[8,2,4,2,80,512]{5,4,3,2,1,0:T(8,128)(2,1)}, bf16[2,640,1024]{2,1,0:T(8,128)(2,1)S(1)}) custom-call(bf16[4,128,512]{2,1,0:T(8,128)(2,1)S(1)} %pad_maximum_fusion.mine, bf16[16,128]{1,0:T(8,128)(2,1)S(1)} %pad_maximum_fusion.1.info), custom_call_target="tpu_custom_call" | custom-call | tf_op jit(solution)/shard_map/dispatch/pallas_call | solution.py:254
  114.5 19.2 %experts.1 = (bf16[2,192,2048]{2,1,0:T(8,128)(2,1)}, bf16[2,192,2048]{2,1,0:T(8,128)(2,1)}, bf16[2,192,2048]{2,1,0:T(8,128)(2,1)}, bf16[4,2,640,512]{3,2,1,0:T(8,128)(2,1)}, bf16[2,16,640]{2,1,0:T(8,128)(2,1)}) custom-call(bf16[8,2,640,512]{3,2,1,0:T(8,128)(2,1)} %bitcast.95, bf16[2,192,2048]{2,1,0:T(8,128)(2,1)} %w_gate.1, bf16[2,192,2048]{2,1,0:T(8,128)(2,1)} %w_up.1, ...), custom_call_target="tpu_custom_call" | custom-call | flops 8000000000 | bytes 25000000 | tf_op jit(solution)/shard_map/experts/pallas_call | solution.py:319
  133.8 2.9 fusion.8
  136.7 0.2 slice_bitcast_fusion.1
  136.9 0.3 collective-permute-start
  137.1 3.1 collective-permute-start.1
  140.2 28.5 %collective-permute-done = bf16[2,640,512]{2,1,0:T(8,128)(2,1)S(1)} collective-permute-done((bf16[2,640,512]{2,1,0:T(8,128)(2,1)S(1)}, bf16[2,640,512]{2,1,0:T(8,128)(2,1)S(1)}, u32[]{:S(2)}, u32[]{:S(2)}) %collective-permute-start) | collective-permute-done | bytes 1310752 | tf_op jit(solution)/shard_map/ppermute | solution.py:369
  168.7 1.2 add_convert_fusion
  169.9 1.7 copy.81
  171.6 5.7 %all-to-all-start = ((bf16[2,2,4,2,80,512]{5,4,1,0,3,2:T(8,128)(2,1)}), bf16[2,2,4,2,80,512]{5,4,1,0,3,2:T(8,128)(2,1)}, u32[]{:S(2)}, u32[]{:S(2)}) async-start(bf16[2,2,4,2,80,512]{5,4,1,0,3,2:T(8,128)(2,1)} %copy.81), calls=%async_computation | async-start | bytes 5242880 | tf_op jit(solution)/shard_map/all_to_all | solution.py:373
  177.2 2.2 copy.106
  179.5 27.8 %all-to-all-done = bf16[2,2,4,2,80,512]{5,4,1,0,3,2:T(8,128)(2,1)} async-done(((bf16[2,2,4,2,80,512]{5,4,1,0,3,2:T(8,128)(2,1)}), bf16[2,2,4,2,80,512]{5,4,1,0,3,2:T(8,128)(2,1)}, u32[]{:S(2)}, u32[]{:S(2)}) %all-to-all-start) | async-done | bytes 2621472 | tf_op jit(solution)/shard_map/all_to_all | solution.py:373
  207.2 7.9 %bitcast_convert_fusion = bf16[2,8,128,2,512]{4,2,3,1,0:T(8,128)(2,1)} fusion(bf16[2,4,2,80,8,128,1]{5,4,3,2,1,0,6:T(8,128)(2,1)} %bitcast.71, s32[]{:T(128)S(6)} %select_n.91, bf16[2,2,4,2,80,512]{5,4,1,0,3,2:T(8,128)(2,1)} %all-to-all-done), kind=kOutput, calls=%fused_computation | convolution fusion | flops 2687762432 | bytes 9437188 | tf_op jit(solution)/shard_map/gyljst,qlygjd->gstqd/dot_general | solution.py:342
  215.2 6.2 %copy.85 = bf16[2,8,128,2,512]{2,4,3,1,0:T(8,128)(2,1)} copy(bf16[2,8,128,2,512]{4,2,3,1,0:T(8,128)(2,1)} %bitcast_convert_fusion) | data formatting | bytes 8388608 | tf_op jit(solution)/shard_map/convert_element_type | solution.py:380
  221.4 1.4 slice_dynamic-update-slice_fusion
  222.9 1.2 slice_dynamic-update-slice_fusion.12
  224.1 1.1 slice_dynamic-update-slice_fusion.10
  225.3 0.1 slice_dynamic-update-slice_fusion.8
  225.3 0.1 slice_dynamic-update-slice_fusion.6
  225.4 0.1 slice_dynamic-update-slice_fusion.4
  225.5 0.1 slice_dynamic-update-slice_fusion.2
  225.6 0.1 slice_dynamic-update-slice_fusion.1
  225.7 0.1 slice_dynamic-update-slice_fusion.13
  226.2 2.3 constant_dynamic-slice_fusion.1
  228.5 6.5 %copy.86 = bf16[8,2,128,1024]{3,2,1,0:T(8,128)(2,1)} copy(bf16[8,2,128,1024]{2,3,1,0:T(8,128)(2,1)} %constant_dynamic-slice_fusion.1) | data formatting | bytes 8388608 | tf_op jit(solution)/shard_map/jit(_roll_dynamic)/dynamic_slice | solution.py:382
  234.9 0.9 slice_reduce_fusion
  235.8 0.1 reshape_squeeze.3
  235.9 0.6 copy.88
  236.5 4.7 %all-to-all-start.1 = ((bf16[2,4,2,80]{3,2,0,1:T(2,128)(2,1)}), bf16[2,4,2,80]{3,2,0,1:T(2,128)(2,1)S(1)}, u32[]{:S(2)}, u32[]{:S(2)}) async-start(bf16[2,4,2,80]{3,2,0,1:T(2,128)(2,1)} %copy.88), calls=%async_computation.2 | async-start | bytes 8192 | tf_op jit(solution)/shard_map/all_to_all | solution.py:377
  241.3 3.8 %all-to-all-done.1 = bf16[2,4,2,80]{3,2,0,1:T(2,128)(2,1)S(1)} async-done(((bf16[2,4,2,80]{3,2,0,1:T(2,128)(2,1)}), bf16[2,4,2,80]{3,2,0,1:T(2,128)(2,1)S(1)}, u32[]{:S(2)}, u32[]{:S(2)}) %all-to-all-start.1) | async-done | bytes 2592 | tf_op jit(solution)/shard_map/all_to_all | solution.py:377
  245.1 0.5 fusion.2
  245.9 0.1 fusion.4
  246.0 12.0 %all_to_all.15 = bf16[16,8,128]{2,1,0:T(8,128)(2,1)S(1)} all-to-all(bf16[16,8,128]{2,1,0:T(8,128)(2,1)S(1)} %bitcast.93), channel_id=1, replica_groups=mesh['y'=4,'z'=8,'c'=2,'x'=4] {'z','c'}, dimensions={0} | all-to-all | bytes 65536 | tf_op jit(solution)/shard_map/all_to_all | solution.py:386
  258.1 0.7 copy.91
  258.8 36.9 %reduce-scatter.2.cloned.1.call-done = bf16[1,128,1024]{2,1,0:T(8,128)(2,1)} async-done(((bf16[16,128,1024]{2,1,0:T(8,128)(2,1)}), bf16[1,128,1024]{2,1,0:T(8,128)(2,1)}) %reduce-scatter.2.cloned.1.call-update) | async-done | bytes 262160 | tf_op jit(solution)/shard_map/reduce_scatter | solution.py:383
  295.7 1.9 pad_select_fusion
  297.7 0.1 copy.87
  297.8 0.1 copy.93
  297.9 2.0 all-reduce.7.cloned.1.call-done
  299.9 0.9 copy.92
  300.9 0.4 select_reduce_fusion
  301.3 0.7 copy.94
  301.9 49.2 %all-reduce.5.cloned.1.call-done = bf16[128,2048]{1,0:T(8,128)(2,1)} async-done(((bf16[128,2048]{1,0:T(8,128)(2,1)}), bf16[128,2048]{1,0:T(8,128)(2,1)}) %all-reduce.5.cloned.1.call-update) | async-done | bytes 524304 | tf_op jit(solution)/shard_map/psum | solution.py:390
  351.2 1.9 copy.154
  (43 shorter events, 0.8 us)
Async XLA Ops:
  136.7 32.0 %copy-start.1 = (bf16[4,2,640,512]{3,2,1,0:T(8,128)(2,1)S(1)}, bf16[4,2,640,512]{3,2,1,0:T(8,128)(2,1)}, u32[]{:S(2)}) copy-start(bf16[4,2,640,512]{3,2,1,0:T(8,128)(2,1)} %get-tuple-element.14) | copy-start | bytes 15728644
  136.9 31.8 %collective-permute-start = (bf16[2,640,512]{2,1,0:T(8,128)(2,1)S(1)}, bf16[2,640,512]{2,1,0:T(8,128)(2,1)S(1)}, u32[]{:S(2)}, u32[]{:S(2)}) collective-permute-start(bf16[2,640,512]{2,1,0:T(8,128)(2,1)S(1)} %get-tuple-element.26), channel_id=1, source_target_pairs={{0,1},{1,2},{2,3},{3,0},{4,5},{5,6},{6,7},{7,4},{8,9},{9,10},{10,1... | collective-permute-start | bytes 3932168 | tf_op jit(solution)/shard_map/ppermute | solution.py:369
  137.1 31.6 %collective-permute-start.1 = (bf16[2,640,512]{2,1,0:T(8,128)(2,1)S(1)}, bf16[2,640,512]{2,1,0:T(8,128)(2,1)S(1)}, u32[]{:S(2)}, u32[]{:S(2)}) collective-permute-start(bf16[2,640,512]{2,1,0:T(8,128)(2,1)S(1)} %get-tuple-element.27), channel_id=1, source_target_pairs={{0,3},{1,0},{2,1},{3,2},{4,7},{5,4},{6,5},{7,6},{8,11},{9,8},{10,9... | collective-permute-start | bytes 3932168 | tf_op jit(solution)/shard_map/ppermute | solution.py:370
  171.6 35.7 %all-to-all-start = ((bf16[2,2,4,2,80,512]{5,4,1,0,3,2:T(8,128)(2,1)}), bf16[2,2,4,2,80,512]{5,4,1,0,3,2:T(8,128)(2,1)}, u32[]{:S(2)}, u32[]{:S(2)}) async-start(bf16[2,2,4,2,80,512]{5,4,1,0,3,2:T(8,128)(2,1)} %copy.81), calls=%async_computation | async-start | bytes 5242880 | tf_op jit(solution)/shard_map/all_to_all | solution.py:373
  177.2 118.5 %reduce-scatter.2.cloned.1.call-start = ((), (), s32[]{:S(2)}) async-start(), calls=%async_computation.4 | async-start | bytes 4456448 | tf_op jit(solution)/shard_map/reduce_scatter | solution.py:383
  221.4 3.8 %copy-start = (bf16[2,8,128,2,512]{2,4,3,1,0:T(8,128)(2,1)S(1)}, bf16[2,8,128,2,512]{2,4,3,1,0:T(8,128)(2,1)}, u32[]{:S(2)}) copy-start(bf16[2,8,128,2,512]{2,4,3,1,0:T(8,128)(2,1)} %copy.85) | copy-start | bytes 12582916
  234.9 10.2 %copy-start.2 = (bf16[160,8,8,128]{3,2,1,0:T(8,128)(2,1)S(1)}, bf16[160,8,8,128]{3,2,1,0:T(8,128)(2,1)}, u32[]{:S(2)}) copy-start(bf16[160,8,8,128]{3,2,1,0:T(8,128)(2,1)} %copy.106) | copy-start | bytes 7864324
  234.9 62.8 %copy-start.3 = (s32[128,8]{0,1:T(8,128)S(1)}, s32[128,8]{0,1:T(8,128)}, u32[]{:S(2)}) copy-start(s32[128,8]{0,1:T(8,128)} %param.9) | copy-start | bytes 12292
  234.9 62.9 %copy-start.4 = (bf16[128,8]{0,1:T(8,128)(2,1)S(1)}, bf16[128,8]{0,1:T(8,128)(2,1)}, u32[]{:S(2)}) copy-start(bf16[128,8]{0,1:T(8,128)(2,1)} %param.10) | copy-start | bytes 6148
  236.5 8.6 %all-to-all-start.1 = ((bf16[2,4,2,80]{3,2,0,1:T(2,128)(2,1)}), bf16[2,4,2,80]{3,2,0,1:T(2,128)(2,1)S(1)}, u32[]{:S(2)}, u32[]{:S(2)}) async-start(bf16[2,4,2,80]{3,2,0,1:T(2,128)(2,1)} %copy.88), calls=%async_computation.2 | async-start | bytes 8192 | tf_op jit(solution)/shard_map/all_to_all | solution.py:377
  241.3 58.7 %all-reduce.7.cloned.1.call-start = ((), (), s32[]{:S(2)}) async-start(), calls=%async_computation.6 | async-start | bytes 131072 | tf_op jit(solution)/shard_map/psum | solution.py:387
  258.8 92.4 %all-reduce.5.cloned.1.call-start = ((), (), s32[]{:S(2)}) async-start(), calls=%async_computation.5 | async-start | bytes 1048576 | tf_op jit(solution)/shard_map/psum | solution.py:390
Sparse Core Ops, SparseCore 0:
  235.1 60.6 reduce-scatter.1
Sparse Core Ops, SparseCore 1:
  258.9 41.0 all-reduce.6
  302.8 48.3 all-reduce.4
where the time goes:
time: 361 us; the launch traced here: 360 us
  waiting for transfers between devices  148 us (41%)
  Pallas kernels  123 us (34%)
  local copies, waits for them, and re-layouts  31 us (9%)
  between operations  15.8 us (4%)
  starting transfers between devices  13.7 us (4%)
  blocking collectives  12 us (3%)
  matrix products  8.4 us (2%)
  other arithmetic  7.99 us (2%)
    pallas_call x1, Pallas kernels, dispatch(): pl.pallas_call(dispatch_kernel, out_shape=(jax.ShapeDtypeStruct((8, LE, N...  104 us
    psum x1, waiting for transfers between devices, body(): grad_tokens = lax.psum(wide, 'x')  49.2 us
    reduce_scatter x1, waiting for transfers between devices, body(): home = lax.psum_scatter(home, ('z', 'c'), scatter_dimension=0, tiled=False)  36.9 us
    ppermute x1, waiting for transfers between devices, body(): got0 = lax.ppermute(give[:, 0], 'x', up_ring)  28.5 us
    all_to_all x1, waiting for transfers between devices, body(): kept = lax.all_to_all(kept, 'y', split_axis=2, concat_axis=2, tiled=True)  27.8 us
    pallas_call x1, Pallas kernels, experts(): pl.pallas_call(expert_kernel, grid=(le,), out_shape=(jax.ShapeDtypeStruct...  19.2 us
    all_to_all x1, blocking collectives, body(): lax.all_to_all(ptok, ('z', 'c'), split_axis=0, concat_axis=0, tiled=True)  12 us
    unnamed x40, local copies, waits for them, and re-layouts  9.6 us
  transfers between devices with their start and end apart: 7, of which 6 were waited for; matrix products, arithmetic and copies ran while one was open for 3% of the time, Pallas kernels for 0%

commit v1 on v0

--- a/solution.py
+++ b/solution.py
@@ -13,6 +13,7 @@
 TOK = 128
 GROUP = 4 * NC * SLOTS
 LANES = 512
+WIDE = 256
 BF = jnp.bfloat16
 F32 = jnp.float32
 MESH = pl.DeviceIdType.MESH
@@ -30,8 +31,8 @@
 
 
 def dispatch_kernel(
-    mine, info, rows, pick_out,
-    blocks, infos, pick_w, out_y, relay,
+    mine, info, rows, goals,
+    blocks, infos, pick, pick_w, out_y, relay,
     i_send, i_recv, z_send, z_recv, p_send, p_recv, y_send, y_recv, r_send, r_recv, x_send, x_recv, l_sem, s_sem,
 ):
     y, z, c, x = axes()
@@ -145,7 +146,7 @@
             remote(
                 mine.at[k], blocks.at[k, at, other], p_send.at[k, at], p_recv.at[k, at], c=other
             ).wait_recv()
-        chosen = pick_out[g] if k < 2 else pick_w[g]
+        chosen = pick[g] if k < 2 else pick_w[g]
         got = jnp.dot(
             chosen,
             blocks[k, 4 * g : 4 * g + 4].reshape(4 * NC * TOK, LANES),
@@ -206,10 +207,11 @@
         goal = jnp.where(
             hits[s] > 0, ranks[s * NY * LE : (s + 1) * NY * LE] + float(SLOTS * i), -1.0
         )
+        goals[s] = goal
         for e in range(NY * LE):
             same = slot_row == goal[e : e + 1]
             at = (g, pl.ds(e * GROUP, GROUP), pl.ds(i * TOK, TOK))
-            pick_out[at] = jnp.where(same, 1.0, 0.0).astype(BF)
+            pick[at] = jnp.where(same, 1.0, 0.0).astype(BF)
             pick_w[at] = jnp.where(same, weights[s][e : e + 1], 0.0).astype(BF)
 
     for k in range(4):
@@ -255,13 +257,14 @@
         dispatch_kernel,
         out_shape=(
             jax.ShapeDtypeStruct((8, LE, NY, 2, GROUP, LANES), BF),
-            jax.ShapeDtypeStruct((2, NY * LE * GROUP, 4 * NC * TOK), BF),
+            jax.ShapeDtypeStruct((NZ * NC, NY * LE, TOK), F32),
         ),
         in_specs=[vmem, vmem],
         out_specs=(anyw, vmem),
         scratch_shapes=[
             pltpu.VMEM((4, NZ, NC, TOK, LANES), BF),
             pltpu.VMEM((NZ, NC, 16, TOK), BF),
+            pltpu.VMEM((2, NY * LE * GROUP, 4 * NC * TOK), BF),
             pltpu.VMEM((2, NY * LE * GROUP, 4 * NC * TOK), BF),
             pltpu.VMEM((4, 2, NY, LE, GROUP, LANES), BF),
             pltpu.VMEM((4, 2, LE, GROUP, LANES), BF),
@@ -301,15 +304,22 @@
     d_gate = (back * up * sig * (1.0 + gate * (1.0 - sig))).astype(BF)
     d_up = (back * act).astype(BF)
     product = (hidden.astype(F32) * back).astype(BF)
-    probs[0] = nt(jnp.ones((16, product.shape[1]), BF), product).astype(BF)
+    ones = jnp.ones((16, product.shape[1]), BF)
+    probs[...] = jnp.zeros_like(probs)
+    for yy in range(NY):
+        for g in range(2):
+            at = (2 * yy + g) * GROUP
+            probs[0, yy, g, :, 0:GROUP] = nt(ones, product[at : at + GROUP]).astype(BF)
     for q in range(4):
         g_down[0, :, cut(q)] = tn(hidden, rows[4 + q, 0]).astype(BF)
         g_gate[0, :, cut(q)] = tn(d_gate, rows[q, 0]).astype(BF)
         g_up[0, :, cut(q)] = tn(d_up, rows[q, 0]).astype(BF)
-        part[q, 0] = (
+        sent = (
             jnp.dot(d_gate, w_gate[0, :, cut(q)], preferred_element_type=F32)
             + jnp.dot(d_up, w_up[0, :, cut(q)], preferred_element_type=F32)
         ).astype(BF)
+        part[2 * q, 0] = sent[:, :WIDE]
+        part[2 * q + 1, 0] = sent[:, WIDE:]
 
 
 def experts(rows, w_gate, w_up, w_down):
@@ -323,14 +333,14 @@
             jax.ShapeDtypeStruct((le, hid, width), BF),
             jax.ShapeDtypeStruct((le, hid, width), BF),
             jax.ShapeDtypeStruct((le, hid, width), BF),
-            jax.ShapeDtypeStruct((4, le, n, LANES), BF),
-            jax.ShapeDtypeStruct((le, 16, n), BF),
+            jax.ShapeDtypeStruct((8, le, n, WIDE), BF),
+            jax.ShapeDtypeStruct((le, NY, 2, 16, TOK), BF),
         ),
         in_specs=[pl.BlockSpec((8, 1, n, LANES), lambda i: (0, i, 0, 0)), weight, weight, weight],
         out_specs=(
             weight, weight, weight,
-            pl.BlockSpec((4, 1, n, LANES), lambda i: (0, i, 0, 0)),
-            pl.BlockSpec((1, 16, n), lambda i: (i, 0, 0)),
+            pl.BlockSpec((8, 1, n, WIDE), lambda i: (0, i, 0, 0)),
+            pl.BlockSpec((1, NY, 2, 16, TOK), lambda i: (i, 0, 0, 0, 0)),
         ),
         compiler_params=pltpu.CompilerParams(vmem_limit_bytes=56 << 20),
         cost_estimate=pl.CostEstimate(flops=8_000_000_000, bytes_accessed=25_000_000, transcendentals=250_000),
@@ -338,61 +348,317 @@
     )(rows, w_gate, w_up, w_down)
 
 
-def dot(spec, a, b):
-    return jnp.einsum(spec, a, b, preferred_element_type=F32)
+def return_kernel(
+    part, probs, goals, info, grads, grad_probs,
+    own, x_in, kept, y_in, relay, pick, pick_t, sums, p_in, z_out, z_in, f_out, f_in, v_out, v_in, b_in, b_all, b_out,
+    o_sem, x_send, x_recv, y_send, y_recv, r_send, r_recv, p_send, p_recv, z_send, z_recv, f_send, f_recv,
+    b_send, b_recv, v_send, v_recv, g_send, g_recv,
+):
+    y, z, c, x = axes()
+    h = x % 2
+    other = 1 - c
+    sign = 1 - 2 * c
+    z_long, z_short = (z + sign + NZ) % NZ, (z - sign + NZ) % NZ
+    y_up, y_down = (y + 1) % NY, (y + NY - 1) % NY
+    x_up, x_down = (x + 1) % NX, (x + NX - 1) % NX
+    x_far = (x + 2) % NX
+
+    barrier = pltpu.get_barrier_semaphore()
+    for m in range(NZ):
+        for cc in ((c, other) if m else (other,)):
+            pl.semaphore_signal(barrier, inc=1, device_id={"z": (z + m) % NZ, "c": cc}, device_id_type=MESH)
+    for m in range(1, NY):
+        pl.semaphore_signal(barrier, inc=1, device_id={"y": (y + m) % NY}, device_id_type=MESH)
+    for m in range(1, NX):
+        pl.semaphore_signal(barrier, inc=1, device_id={"x": (x + m) % NX}, device_id_type=MESH)
+    pl.semaphore_wait(barrier, 2 * NZ - 1 + NY - 1 + NX - 1)
+
+    waits = []
+
+    def go(copy):
+        copy.start()
+        waits.append(copy)
+
+    def x_copy(j, le):
+        return remote(
+            part.at[4 * (1 - h) + j, le], x_in.at[j, le], x_send.at[j, le], x_recv.at[j, le],
+            x=x_up if le == 0 else x_down,
+        )
+
+    def own_copy(j):
+        return pltpu.make_async_copy(part.at[4 * h + j], own.at[j], o_sem.at[j])
+
+    def b_copy(m):
+        return remote(
+            probs.at[:, (y + NY - m) % NY], b_in.at[m], b_send.at[m], b_recv.at[m], y=(y + NY - m) % NY
+        )
+
+    for m in range(1, NY):
+        go(b_copy(m))
+    for j in range(4):
+        for le in range(LE):
+            go(x_copy(j, le))
+        own_copy(j).start()
+    b_own = pltpu.make_async_copy(probs.at[:, y], b_in.at[0], b_send.at[0])
+    b_own.start()
+
+    slot_row = lax.broadcasted_iota(jnp.int32, (GROUP, TOK), 0).astype(F32)
+    same_lane = (
+        lax.broadcasted_iota(jnp.int32, (TOK, TOK), 0) == lax.broadcasted_iota(jnp.int32, (TOK, TOK), 1)
+    ).astype(F32).astype(BF)
+    for s in range(NZ * NC):
+        g, i = s // 8, s % 8
+        goal = goals[s]
+        for e in range(NY * LE):
+            pick[g, pl.ds(e * GROUP, GROUP), pl.ds(i * TOK, TOK)] = jnp.where(
+                slot_row == goal[e : e + 1], 1.0, 0.0
+            ).astype(BF)
+        pick_t[g, pl.ds(i * TOK, TOK), :] = nt(same_lane, pick[g, :, pl.ds(i * TOK, TOK)]).astype(BF)
+
+    def v_copy(at, r, cc, far):
+        back = PLACE[(NZ - r) % NZ]
+        return remote(
+            v_out.at[at, cc], v_in.at[back, c], v_send.at[at, far], v_recv.at[back, c], z=(z + r) % NZ, c=cc
+        )
+
+    b_own.wait()
+    for m in range(1, NY):
+        b_copy(m).wait_recv()
+    lane_row = lax.broadcasted_iota(jnp.int32, (16, 4 * NC * TOK), 0)
+    for g in range(2):
+        values = jnp.zeros((16, 4 * NC * TOK), F32)
+        for e in range(NY * LE):
+            got = jnp.dot(
+                b_in[e // LE, e % LE, g][:, :GROUP],
+                pick[g, pl.ds(e * GROUP, GROUP), :],
+                preferred_element_type=F32,
+            )
+            values = jnp.where(lane_row == e, got, values)
+        values = values.astype(BF)
+        for i in range(8):
+            v_out[4 * g + i // 2, i % 2] = values[:, i * TOK : (i + 1) * TOK]
+    for r in range(NZ):
+        if r:
+            go(v_copy(PLACE[r], r, c, 0))
+        go(v_copy(PLACE[r], r, other, 1))
+
+    def y_copy(j, d, le):
+        src = kept.at[j, le, (y + NY - d) % NY]
+        sems = dict(send=y_send.at[j, d - 1, le], recv=y_recv.at[j, d - 1, le])
+        if d == 1:
+            return remote(src, y_in.at[j, :, 1, le], y=y_down, **sems)
+        if d == 3:
+            return remote(src, y_in.at[j, :, 3, le], y=y_up, **sems)
+        return remote(src, relay.at[j, le], y=y_up if le == 0 else y_down, **sems)
+
+    def relayed(j, le):
+        return remote(
+            relay.at[j, le], y_in.at[j, :, 2, le], r_send.at[j, le], r_recv.at[j, le],
+            y=y_up if le == 0 else y_down,
+        )
+
+    def x_stage(j):
+        own_copy(j).wait()
+        for le in range(LE):
+            x_copy(j, le).wait_recv()
+            kept[j, le] = (own[j, le].astype(F32) + x_in[j, le].astype(F32)).astype(BF)
+            go(y_copy(j, 2, le))
+            go(y_copy(j, 1, le))
+            go(y_copy(j, 3, le))
+            y_in[j, :, 0, le] = kept[j, le, y]
+
+    def relay_stage(j):
+        for le in range(LE):
+            y_copy(j, 2, le).wait_recv()
+            go(relayed(j, le))
+
+    def p_copy(j, g):
+        return remote(
+            sums.at[j, g, other], p_in.at[j, g], p_send.at[j, g], p_recv.at[j, g], c=other
+        )
+
+    def sum_stage(j):
+        for le in range(LE):
+            y_copy(j, 1, le).wait_recv()
+            y_copy(j, 3, le).wait_recv()
+            relayed(j, le).wait_recv()
+        for g in (1, 0):
+            got = jnp.dot(
+                pick_t[g], y_in[j, g].reshape(NY * LE * GROUP, WIDE), preferred_element_type=F32
+            ).astype(BF).reshape(4, NC, TOK, WIDE)
+            for cc in range(NC):
+                sums[j, g, cc] = got[:, cc]
+            go(p_copy(j, g))
+
+    def place(long, s):
+        if s == 0:
+            return 0
+        if long:
+            return 7 if s == 4 else 2 * s - c
+        return 2 * s - 1 + c
+
+    def z_copy(j, long, s):
+        index = (s - 1) if long else (3 + s)
+        return remote(
+            z_out.at[j, index], z_in.at[j, index], z_send.at[j, index], z_recv.at[j, index],
+            z=z_short if long else z_long,
+        )
+
+    def both(j, at):
+        g, i = (0, 0) if isinstance(at, int) and at == 0 else (at // 4, at % 4)
+        return sums[j, g, c, i].astype(F32) + p_in[j, g, i].astype(F32)
+
+    def z_stage(j, s):
+        if s == 4:
+            for g in range(2):
+                p_copy(j, g).wait_recv()
+        for long in ((True, False) if s < 4 else (True,)):
+            index = (s - 1) if long else (3 + s)
+            total = both(j, place(long, s))
+            if s < (4 if long else 3):
+                z_copy(j, long, s + 1).wait_recv()
+                total = total + z_in[j, index + 1].astype(F32)
+            z_out[j, index] = total.astype(BF)
+            go(z_copy(j, long, s))
+
+    def f_copy(j, m):
+        return remote(
+            f_out.at[j], f_in.at[j, m - 1], f_send.at[j, m - 1], f_recv.at[j, m - 1], x=(x + m) % NX
+        )
+
+    def home_stage(j):
+        total = both(j, 0)
+        for long in (True, False):
+            z_copy(j, long, 1).wait_recv()
+            total = total + z_in[j, 0 if long else 4].astype(F32)
+        f_out[j] = total.astype(BF)
+        for m in (2, 1, 3):
+            go(f_copy(j, m))
+
+    def end_stage(j):
+        for m in (1, 3, 2):
+            f_copy(j, m).wait_recv()
+        grads[4 * (1 - h) + j] = (f_in[j, 0].astype(F32) + f_in[j, 2].astype(F32)).astype(BF)
+        grads[4 * h + j] = (f_out[j].astype(F32) + f_in[j, 1].astype(F32)).astype(BF)
+
+    def g_copy(m):
+        return remote(b_out, b_all.at[x], g_send.at[m], g_recv.at[x], x=(x + m) % NX)
+
+    def gate_stage():
+        for at in range(NZ):
+            for far, cc in ((0, c), (1, other)):
+                if at == 0 and far == 0:
+                    continue
+                remote(
+                    v_out.at[at, cc], v_in.at[at, cc], v_send.at[at, far], v_recv.at[at, cc], c=other
+                ).wait_recv()
+        v_in[0, c] = v_out[0, c]
+        row = lax.broadcasted_iota(jnp.int32, (16, TOK), 0)
+        base = (y + row // LE) % NY * (NZ * NC * LE) + row % LE
+        base = jnp.where(row < NY * LE, base, -NZ * NC * LE)
+        found = [jnp.zeros((16, TOK), F32) for _ in range(8)]
+        for r in range(NZ):
+            for cc in range(NC):
+                expert = (base + ((z + r) % NZ * NC + cc) * LE).astype(F32)
+                value = v_in[PLACE[r], cc].astype(F32)
+                for k in range(8):
+                    same = info[k : k + 1].astype(F32) == expert
+                    found[k] = jnp.where(same, value, found[k])
+        for k in range(8):
+            total = jnp.sum(found[k], axis=0, keepdims=True)
+            b_out[k : k + 1] = total.astype(BF)
+            b_out[8 + k : 9 + k] = total.astype(BF)
+        for m in range(1, NX):
+            go(g_copy(m))
+
+    events = []
+    for j in range(4):
+        events += [(2 * j, j, x_stage, (j,)), (2 * j + 1, j, relay_stage, (j,)), (2 * j + 2, j, sum_stage, (j,))]
+        events += [(2 * j + 3 + (4 - s), j, z_stage, (j, s)) for s in (4, 3, 2, 1)]
+        events += [(2 * j + 7, j, home_stage, (j,)), (2 * j + 9, j, end_stage, (j,))]
+    events.append((7.5, 0, gate_stage, ()))
+    for _, _, stage, given in sorted(events, key=lambda e: (e[0], e[1])):
+        stage(*given)
+    b_all[x] = b_out[...]
+    for m in range(1, NX):
+        at = (x + NX - m) % NX
+        remote(b_out, b_all.at[at], g_send.at[m], g_recv.at[at], x=x_up).wait_recv()
+    total = (
+        b_all[0].astype(F32) + b_all[1].astype(F32) + b_all[2].astype(F32) + b_all[3].astype(F32)
+    )
+    grad_probs[...] = total[:8] / info[...].astype(F32)[8:]
+    for copy in waits:
+        copy.wait_send()
+
+
+def give_back(part, probs, goals, info):
+    vmem = pl.BlockSpec(memory_space=pltpu.VMEM)
+    anyw = pl.BlockSpec(memory_space=pl.ANY)
+    dma = pltpu.SemaphoreType.DMA
+    return pl.pallas_call(
+        return_kernel,
+        out_shape=(
+            jax.ShapeDtypeStruct((8, TOK, WIDE), BF),
+            jax.ShapeDtypeStruct((8, TOK), F32),
+        ),
+        in_specs=[anyw, vmem, vmem, vmem],
+        out_specs=(vmem, vmem),
+        scratch_shapes=[
+            pltpu.VMEM((4, LE, NY, 2, GROUP, WIDE), BF),
+            pltpu.VMEM((4, LE, NY, 2, GROUP, WIDE), BF),
+            pltpu.VMEM((4, LE, NY, 2, GROUP, WIDE), BF),
+            pltpu.VMEM((4, 2, NY, LE, GROUP, WIDE), BF),
+            pltpu.VMEM((4, LE, 2, GROUP, WIDE), BF),
+            pltpu.VMEM((2, NY * LE * GROUP, 4 * NC * TOK), BF),
+            pltpu.VMEM((2, 4 * NC * TOK, NY * LE * GROUP), BF),
+            pltpu.VMEM((4, 2, NC, 4, TOK, WIDE), BF),
+            pltpu.VMEM((4, 2, 4, TOK, WIDE), BF),
+            pltpu.VMEM((4, 7, TOK, WIDE), BF),
+            pltpu.VMEM((4, 7, TOK, WIDE), BF),
+            pltpu.VMEM((4, TOK, WIDE), BF),
+            pltpu.VMEM((4, 3, TOK, WIDE), BF),
+            pltpu.VMEM((NZ, NC, 16, TOK), BF),
+            pltpu.VMEM((NZ, NC, 16, TOK), BF),
+            pltpu.VMEM((NY, LE, 2, 16, TOK), BF),
+            pltpu.VMEM((NX, 16, TOK), BF),
+            pltpu.VMEM((16, TOK), BF),
+            dma((4,)),
+            dma((4, LE)), dma((4, LE)),
+            dma((4, 3, LE)), dma((4, 3, LE)),
+            dma((4, LE)), dma((4, LE)),
+            dma((4, 2)), dma((4, 2)),
+            dma((4, 7)), dma((4, 7)),
+            dma((4, 3)), dma((4, 3)),
+            dma((NY,)), dma((NY,)),
+            dma((NZ, 2)), dma((NZ, NC)),
+            dma((NX,)), dma((NX,)),
+        ],
+        compiler_params=pltpu.CompilerParams(
+            collective_id=1, has_side_effects=True, vmem_limit_bytes=48 << 20
+        ),
+        name="give_back",
+    )(part, probs, goals, info)
 
 
 def body(tokens, grad_out, routes, probs, w_gate, w_up, w_down):
-    x = lax.axis_index("x")
-    z = lax.axis_index("z")
-    c = lax.axis_index("c")
-    h = x % 2
-    half = 2 * LANES
-    quarter = LANES
-    tok_rows = TOK
-    le = LE
-    cut = [
-        lax.dynamic_slice_in_dim(a, h * half + q * LANES, LANES, axis=1)
-        for a in (tokens, grad_out)
-        for q in range(2)
-    ]
+    h = lax.axis_index("x") % 2
+    mine = jnp.stack(
+        [
+            lax.dynamic_slice_in_dim(a, h * 2 * LANES + q * LANES, LANES, axis=1)
+            for a in (tokens, grad_out)
+            for q in range(2)
+        ]
+    )
     info = jnp.concatenate([routes.T.astype(BF), probs.T], axis=0)
-    rows, pick = dispatch(jnp.stack(cut), info)
+    rows, goals = dispatch(mine, info)
     g_gate, g_up, g_down, part, prob = experts(
         rows.reshape(8, LE, NY * 2 * GROUP, LANES), w_gate, w_up, w_down
     )
-    up_ring = [(i, (i + 1) % NX) for i in range(NX)]
-    down_ring = [(i, (i + NX - 1) % NX) for i in range(NX)]
-    part = part.reshape(2, 2, LE, NY * 2 * GROUP, LANES)
-    keep = jnp.where(h == 0, part[0], part[1])
-    give = jnp.where(h == 0, part[1], part[0])
-    got0 = lax.ppermute(give[:, 0], "x", up_ring)
-    got1 = lax.ppermute(give[:, 1], "x", down_ring)
-    kept = (keep.astype(F32) + jnp.stack([got0, got1], axis=1).astype(F32)).astype(BF)
-    kept = kept.reshape(2, LE, NY, 2, GROUP, LANES)
-    kept = lax.all_to_all(kept, "y", split_axis=2, concat_axis=2, tiled=True)
-    y = lax.axis_index("y")
-    kept = jnp.roll(kept, -y, axis=2)
-    pr = prob[:, 0].reshape(LE, NY, 2, GROUP)
-    pr = lax.all_to_all(pr, "y", split_axis=1, concat_axis=1, tiled=True)
-    pr = jnp.roll(pr, -y, axis=1)
-    pick6 = pick.reshape(2, NY, LE, GROUP, 4 * NC, TOK)
-    home = dot("gyljst,qlygjd->gstqd", pick6, kept).astype(BF)
-    home = home.reshape(NZ, NC, TOK, half)
-    home = jnp.roll(jnp.stack([home[PLACE[r]] for r in range(NZ)]), z, axis=0).reshape(NZ * NC, TOK, half)
-    home = lax.psum_scatter(home, ("z", "c"), scatter_dimension=0, tiled=False)
-    ptok = dot("gyljst,lygj->gsylt", pick6, pr).astype(BF).reshape(NZ, NC, NY, LE, TOK)
-    ptok = jnp.roll(jnp.roll(jnp.stack([ptok[PLACE[r]] for r in range(NZ)]), z, axis=0), y, axis=2).reshape(NZ * NC, NY * LE, TOK)
-    ptok = lax.all_to_all(ptok, ("z", "c"), split_axis=0, concat_axis=0, tiled=True)
-    ptok = lax.psum(ptok.astype(F32), "x")
-    zeros = jnp.zeros_like(home)
-    wide = jnp.where(h == 0, jnp.concatenate([home, zeros], -1), jnp.concatenate([zeros, home], -1))
-    grad_tokens = lax.psum(wide, "x")
-    by_expert = jnp.transpose(ptok.reshape(NZ * NC, NY, le, tok_rows), (1, 0, 2, 3)).reshape(-1, tok_rows)
-    chosen = routes[:, :, None] == jnp.arange(by_expert.shape[0])[None, None, :]
-    total = jnp.sum(jnp.where(chosen, by_expert.T[:, None, :], 0), axis=-1)
-    grad_probs = (total / probs.astype(F32)).astype(BF)
-    return (grad_tokens, grad_probs, g_gate, g_up, g_down)
+    grads, grad_probs = give_back(
+        part.reshape(8, LE, NY, 2, GROUP, WIDE), prob, goals, info
+    )
+    grad_tokens = jnp.transpose(grads, (1, 0, 2)).reshape(tokens.shape)
+    return (grad_tokens, grad_probs.T.astype(BF), g_gate, g_up, g_down)
 
 
 def solution(mesh):

time: 361 us -> 212 us (0.59)
  waiting for transfers between devices: 148 us -> 0 us
  Pallas kernels: 123 us -> 202 us
  local copies, waits for them, and re-layouts: 31 us -> 5.76 us
  between operations: 15.8 us -> 0.69 us
  starting transfers between devices: 13.7 us -> 0 us
  blocking collectives: 12 us -> 0 us
  matrix products: 8.4 us -> 0 us
  other arithmetic: 7.99 us -> 2.02 us
    pallas_call x0 -> x1, Pallas kernels: none -> 79.2 us  [give_back(): pl.pallas_call(return_kernel, out_shape=(jax.ShapeDtypeStruct((8, TOK, WI...]
    psum x2 -> x0, waiting for transfers between devices: 51.3 us -> none  [the longest x1 49.2 us: body(): grad_tokens = lax.psum(wide, 'x')]
    reduce_scatter x1 -> x0, waiting for transfers between devices: 36.9 us -> none  [body(): home = lax.psum_scatter(home, ('z', 'c'), scatter_dimension=0, tiled=False)]
    all_to_all x2 -> x0, waiting for transfers between devices: 31.6 us -> none  [the longest x1 27.8 us: body(): kept = lax.all_to_all(kept, 'y', split_axis=2, concat_axis=2, tiled=True)]
    ppermute x2 -> x0, waiting for transfers between devices: 28.5 us -> none  [the longest x1 28.5 us: body(): got0 = lax.ppermute(give[:, 0], 'x', up_ring)]
    all_to_all x1 -> x0, blocking collectives: 12 us -> none  [body(): lax.all_to_all(ptok, ('z', 'c'), split_axis=0, concat_axis=0, tiled=True)]
    all_to_all x2 -> x0, starting transfers between devices: 10.4 us -> none  [the longest x1 5.66 us: body(): kept = lax.all_to_all(kept, 'y', split_axis=2, concat_axis=2, tiled=True)]
    dynamic_slice x4 -> x0, local copies, waits for them, and re-layouts: 8.79 us -> none  [the longest x2 8.73 us: body(): jnp.roll(jnp.stack([home[PLACE[r]] for r in range(NZ)]), z, axis=0)]
  transfers between devices with their start and end apart: 7 -> 0, of which waited for: 6 -> 0; matrix products, arithmetic and copies ran while one was open for 3% -> 0% of each run, Pallas kernels for 0% -> 0%
where the time goes in v1:
time: 212 us; the launch traced here: 211 us
  Pallas kernels  202 us (95%)
  local copies, waits for them, and re-layouts  5.76 us (3%)
    pallas_call x1, Pallas kernels, dispatch(): pl.pallas_call(dispatch_kernel, out_shape=(jax.ShapeDtypeStruct((8, LE, N...  104 us
    pallas_call x1, Pallas kernels, give_back(): pl.pallas_call(return_kernel, out_shape=(jax.ShapeDtypeStruct((8, TOK, WI...  79.2 us
    pallas_call x1, Pallas kernels, experts(): pl.pallas_call(expert_kernel, grid=(le,), out_shape=(jax.ShapeDtypeStruct...  19.3 us
    unnamed x5, local copies, waits for them, and re-layouts  4.34 us

profile of v1, /device:TPU:8, one launch (start us, length us, event | category | flops | bytes accessed | tf_op | source)
XLA Modules:
  0.0 210.9 jit_solution(17608541189855015964)
XLA Ops:
  0.7 0.7 convert_bitcast_fusion.1
  1.3 0.7 pad_maximum_fusion.1.info
  2.0 1.1 dynamic-slice_bitcast_fusion.1
  3.2 0.1 pad_maximum_fusion.mine
  3.2 103.9 %dispatch.1 = (bf16[8,2,4,2,80,512]{5,4,3,2,1,0:T(8,128)(2,1)}, f32[16,8,128]{2,1,0:T(8,128)S(1)}) custom-call(bf16[4,128,512]{2,1,0:T(8,128)(2,1)S(1)} %pad_maximum_fusion.mine, bf16[16,128]{1,0:T(8,128)(2,1)S(1)} %pad_maximum_fusion.1.info), custom_call_target="tpu_custom_call" | custom-call | tf_op jit(solution)/shard_map/dispatch/pallas_call | solution.py:256
  107.2 19.3 %experts.1 = (bf16[2,192,2048]{2,1,0:T(8,128)(2,1)}, bf16[2,192,2048]{2,1,0:T(8,128)(2,1)}, bf16[2,192,2048]{2,1,0:T(8,128)(2,1)}, bf16[8,2,640,256]{3,2,1,0:T(8,128)(2,1)}, bf16[2,4,2,16,128]{4,3,2,1,0:T(8,128)(2,1)}) custom-call(bf16[8,2,640,512]{3,2,1,0:T(8,128)(2,1)} %bitcast.21, bf16[2,192,2048]{2,1,0:T(8,128)(2,1)} %w_gate.1, ...), custom_call_target="tpu_custom_call" | custom-call | flops 8000000000 | bytes 25000000 | tf_op jit(solution)/shard_map/experts/pallas_call | solution.py:329
  126.5 0.0 copy-start
  126.5 2.5 %copy-done = bf16[8,2,640,256]{3,2,1,0:T(8,128)(2,1)S(1)} copy-done((bf16[8,2,640,256]{3,2,1,0:T(8,128)(2,1)S(1)}, bf16[8,2,640,256]{3,2,1,0:T(8,128)(2,1)}, u32[]{:S(2)}) %copy-start) | copy-done | bytes 5242904
  129.0 0.0 copy-start.1
  129.0 0.8 copy-done.1
  129.8 79.2 %give_back.1 = (bf16[8,128,256]{2,1,0:T(8,128)(2,1)S(1)}, f32[8,128]{1,0:T(8,128)S(1)}) custom-call(bf16[8,2,4,2,80,256]{5,4,3,2,1,0:T(8,128)(2,1)S(1)} %bitcast.17, bf16[2,4,2,16,128]{4,3,2,1,0:T(8,128)(2,1)S(1)} %copy-done.1, f32[16,8,128]{2,1,0:T(8,128)S(1)} %get-tuple-element.17.goals, bf16[16,128]{1,0:T(8,128)(2,1)S(1)} %pad_maximum_fusion.1.info), custom_call_target="tpu_custom_call" | custom-call | tf_op jit(solution)/shard_map/give_back/pallas_call | solution.py:598
  209.0 0.3 copy.12
  209.3 1.0 copy.13
  210.3 0.6 convert_bitcast_fusion
Async XLA Ops:
  126.5 2.5 %copy-start = (bf16[8,2,640,256]{3,2,1,0:T(8,128)(2,1)S(1)}, bf16[8,2,640,256]{3,2,1,0:T(8,128)(2,1)}, u32[]{:S(2)}) copy-start(bf16[8,2,640,256]{3,2,1,0:T(8,128)(2,1)} %get-tuple-element.15) | copy-start | bytes 15728644
  129.0 0.8 copy-start.1

commit v2 on v1

--- a/solution.py
+++ b/solution.py
@@ -1,5 +1,3 @@
-import functools
-
 import jax
 import jax.numpy as jnp
 from jax import lax
@@ -26,14 +24,18 @@
     )
 
 
+def nt(a, b):
+    return lax.dot_general(a, b, (((1,), (1,)), ((), ())), preferred_element_type=F32)
+
+
 def axes():
     return tuple(lax.axis_index(n) for n in ("y", "z", "c", "x"))
 
 
 def dispatch_kernel(
-    mine, info, rows, goals,
-    blocks, infos, pick, pick_w, out_y, relay,
-    i_send, i_recv, z_send, z_recv, p_send, p_recv, y_send, y_recv, r_send, r_recv, x_send, x_recv, l_sem, s_sem,
+    mine, info, w_gate, w_up, w_down, rows_out, pick_out, pick_t_out, inner, probs,
+    rows, held, acc, blocks, infos, pick, pick_t, pick_w, out_y, relay,
+    i_send, i_recv, z_send, z_recv, p_send, p_recv, y_send, y_recv, r_send, r_recv, x_send, x_recv, l_sem, w_sem, o_sem, t_sem,
 ):
     y, z, c, x = axes()
     h = x % 2
@@ -51,6 +53,17 @@
         pl.semaphore_signal(barrier, inc=1, device_id={"y": yy}, device_id_type=MESH)
     for xx in (x_up, x_down):
         pl.semaphore_signal(barrier, inc=1, device_id={"x": xx}, device_id_type=MESH)
+    loads = [
+        pltpu.make_async_copy(w.at[le, :, pl.ds(q * LANES, LANES)], held.at[i, le, q], w_sem.at[i, le, q])
+        for i, w in enumerate((w_gate, w_up, w_down))
+        for le in range(LE)
+        for q in range(4)
+    ]
+    for copy in loads:
+        copy.start()
+    pick[...] = jnp.zeros_like(pick)
+    pick_w[...] = jnp.zeros_like(pick_w)
+    acc[...] = jnp.zeros_like(acc)
     pl.semaphore_wait(barrier, 2 * NZ - 1 + 4)
 
     waits = []
@@ -133,11 +146,49 @@
             src, there, x_send.at[k, g, d, le], x_recv.at[k, g, d, le], x=x_up if le == 0 else x_down
         )
 
-    def own_piece(k, g, le):
-        slot = 4 * (k // 2) + 2 * h + k % 2
-        return pltpu.make_async_copy(
-            out_y.at[k, g, 0, le], rows.at[slot, le, y, g], s_sem.at[k, g, le]
-        )
+    def slot_of(k, half):
+        return 4 * (k // 2) + 2 * half + k % 2
+
+    def absorb(k, half):
+        quarter = 2 * half + k % 2
+        slot = slot_of(k, half)
+        for le in range(LE):
+            some = rows[slot, le].reshape(NY * 2 * GROUP, LANES)
+            for i in (0, 1) if k < 2 else (2,):
+                acc[le, i] += nt(some, held[i, le, quarter])
+        pltpu.make_async_copy(rows.at[slot], rows_out.at[slot], o_sem.at[slot]).start()
+
+    def x_landed(k):
+        for g in range(2):
+            for le in range(LE):
+                for d in range(NY):
+                    there = rows.at[slot_of(k, 1 - h), le, (y + NY - d) % NY, g]
+                    remote(
+                        there, there, x_send.at[k, g, d, le], x_recv.at[k, g, d, le],
+                        x=x_up if le == 0 else x_down,
+                    ).wait_recv()
+
+    def activate():
+        for le in range(LE):
+            gate, up = acc[le, 0], acc[le, 1]
+            sig = 1.0 / (1.0 + jnp.exp(-gate))
+            act = gate * sig
+            inner[le, 0] = (act * up).astype(BF)
+            acc[le, 0] = up * sig * (1.0 + gate * (1.0 - sig))
+            acc[le, 1] = act
+
+    def finish():
+        probs[...] = jnp.zeros_like(probs)
+        ones = jnp.ones((16, acc.shape[3]), BF)
+        for le in range(LE):
+            back = acc[le, 2]
+            inner[le, 1] = (back * acc[le, 0]).astype(BF)
+            inner[le, 2] = (back * acc[le, 1]).astype(BF)
+            product = (inner[le, 0].astype(F32) * back).astype(BF)
+            for yy in range(NY):
+                for g in range(2):
+                    at = (2 * yy + g) * GROUP
+                    probs[le, yy, g, :, 0:GROUP] = nt(ones, product[at : at + GROUP]).astype(BF)
 
     def pick_rows(k, g):
         if k in keeps:
@@ -160,7 +211,8 @@
             go(y_piece(k, g, 3, le))
         for le in range(LE):
             go(x_piece(k, g, 0, le))
-            own_piece(k, g, le).start()
+        for le in range(LE):
+            rows[slot_of(k, h), le, y, g] = out_y[k, g, 0, le]
 
     def y_step(k, g):
         for le in range(LE):
@@ -201,55 +253,74 @@
             hits.append(hit)
             weights.append(weight)
     ranks = jnp.dot(jnp.concatenate(hits, axis=0).astype(BF), before, preferred_element_type=F32)
-    slot_row = lax.broadcasted_iota(jnp.int32, (GROUP, TOK), 0).astype(F32)
+    slot_row = lax.broadcasted_iota(jnp.int32, (16, TOK), 0).astype(F32)
     for s in range(NZ * NC):
         g, i = s // 8, s % 8
+        first, last = SLOTS * i // 16, (SLOTS * i + SLOTS - 1) // 16
         goal = jnp.where(
             hits[s] > 0, ranks[s * NY * LE : (s + 1) * NY * LE] + float(SLOTS * i), -1.0
         )
-        goals[s] = goal
         for e in range(NY * LE):
-            same = slot_row == goal[e : e + 1]
-            at = (g, pl.ds(e * GROUP, GROUP), pl.ds(i * TOK, TOK))
-            pick[at] = jnp.where(same, 1.0, 0.0).astype(BF)
-            pick_w[at] = jnp.where(same, weights[s][e : e + 1], 0.0).astype(BF)
-
+            for tile in range(first, last + 1):
+                same = slot_row == goal[e : e + 1] - float(16 * tile)
+                at = (g, pl.ds(e * GROUP + 16 * tile, 16), pl.ds(i * TOK, TOK))
+                pick[at] = jnp.where(same, 1.0, 0.0).astype(BF)
+                pick_w[at] = jnp.where(same, weights[s][e : e + 1], 0.0).astype(BF)
+
+    def pick_copies():
+        return [
+            pltpu.make_async_copy(pick, pick_out, t_sem.at[0]),
+            pltpu.make_async_copy(pick_t, pick_t_out, t_sem.at[1]),
+        ]
+
+    def turn(g):
+        same_lane = (
+            lax.broadcasted_iota(jnp.int32, (TOK, TOK), 0) == lax.broadcasted_iota(jnp.int32, (TOK, TOK), 1)
+        ).astype(F32).astype(BF)
+        for i in range(8):
+            at = pl.ds(i * TOK, TOK)
+            pick_t[g, at, :] = nt(same_lane, pick[g, :, at]).astype(BF)
+        if g:
+            for copy in pick_copies():
+                copy.start()
+
+    def begin(k):
+        keeps[k] = start_chunk(k)
+
+    def ready():
+        for copy in loads:
+            copy.wait()
+
+    def other_half(k):
+        x_landed(k)
+        absorb(k, 1 - h)
+
+    events = [(16.0, ready, ()), (16.1, turn, (0,)), (21.0, turn, (1,))]
     for k in range(4):
-        z_step(k, 1)
+        events += [(10 * k + 5 * n - 2, z_step, (k, n)) for n in (1, 2, 3, 4)]
+        events += [(10 * k + 8.5, pick_rows, (k, 0)), (10 * k + 18.5, pick_rows, (k, 1))]
         if k:
-            y_step(k - 1, 0)
-        z_step(k, 2)
-        if k < 3:
-            keeps[k + 1] = start_chunk(k + 1)
-        pick_rows(k, 0)
-        z_step(k, 3)
-        if k:
-            y_last(k - 1, 0)
-            y_step(k - 1, 1)
-        z_step(k, 4)
-        pick_rows(k, 1)
-        if k:
-            y_last(k - 1, 1)
-    y_step(3, 0)
-    y_last(3, 0)
-    y_step(3, 1)
-    y_last(3, 1)
-    for k in range(4):
+            events.append((10 * k - 1.9, begin, (k,)))
         for g in range(2):
-            for le in range(LE):
-                own_piece(k, g, le).wait()
-                for d in range(NY):
-                    slot = 4 * (k // 2) + 2 * (1 - h) + k % 2
-                    there = rows.at[slot, le, (y + NY - d) % NY, g]
-                    remote(
-                        there, there, x_send.at[k, g, d, le], x_recv.at[k, g, d, le],
-                        x=x_up if le == 0 else x_down,
-                    ).wait_recv()
+            n = 2 * k + g
+            events += [(15 + 7.5 * n, y_step, (k, g)), (18.2 + 7.5 * n, y_last, (k, g))]
+        end = 18.2 + 7.5 * (2 * k + 1)
+        events += [(end + 0.1, absorb, (k, h)), (end + 6, other_half, (k,))]
+    events.append((18.2 + 7.5 * 3 + 6.1, activate, ()))
+    for _, stage, given in sorted(events, key=lambda e: e[0]):
+        stage(*given)
+    finish()
+    for slot in range(8):
+        pltpu.make_async_copy(rows.at[slot], rows_out.at[slot], o_sem.at[slot]).wait()
+    for copy in pick_copies():
+        copy.wait()
     for copy in waits:
         copy.wait_send()
 
 
-def dispatch(mine, info):
+def dispatch(mine, info, w_gate, w_up, w_down):
+    hid = w_gate.shape[1]
+    count = NY * 2 * GROUP
     vmem = pl.BlockSpec(memory_space=pltpu.VMEM)
     anyw = pl.BlockSpec(memory_space=pl.ANY)
     dma = pltpu.SemaphoreType.DMA
@@ -257,14 +328,21 @@
         dispatch_kernel,
         out_shape=(
             jax.ShapeDtypeStruct((8, LE, NY, 2, GROUP, LANES), BF),
-            jax.ShapeDtypeStruct((NZ * NC, NY * LE, TOK), F32),
+            jax.ShapeDtypeStruct((2, NY * LE * GROUP, 4 * NC * TOK), BF),
+            jax.ShapeDtypeStruct((2, 4 * NC * TOK, NY * LE * GROUP), BF),
+            jax.ShapeDtypeStruct((LE, 3, count, hid), BF),
+            jax.ShapeDtypeStruct((LE, NY, 2, 16, TOK), BF),
         ),
-        in_specs=[vmem, vmem],
-        out_specs=(anyw, vmem),
+        in_specs=[vmem, vmem, anyw, anyw, anyw],
+        out_specs=(anyw, anyw, anyw, vmem, vmem),
         scratch_shapes=[
+            pltpu.VMEM((8, LE, NY, 2, GROUP, LANES), BF),
+            pltpu.VMEM((3, LE, 4, hid, LANES), BF),
+            pltpu.VMEM((LE, 3, count, hid), F32),
             pltpu.VMEM((4, NZ, NC, TOK, LANES), BF),
             pltpu.VMEM((NZ, NC, 16, TOK), BF),
             pltpu.VMEM((2, NY * LE * GROUP, 4 * NC * TOK), BF),
+            pltpu.VMEM((2, 4 * NC * TOK, NY * LE * GROUP), BF),
             pltpu.VMEM((2, NY * LE * GROUP, 4 * NC * TOK), BF),
             pltpu.VMEM((4, 2, NY, LE, GROUP, LANES), BF),
             pltpu.VMEM((4, 2, LE, GROUP, LANES), BF),
@@ -274,85 +352,20 @@
             dma((4, 2, 3, LE)), dma((4, 2, 3, LE)),
             dma((4, 2, LE)), dma((4, 2, LE)),
             dma((4, 2, NY, LE)), dma((4, 2, NY, LE)),
-            dma((4,)), dma((4, 2, LE)),
+            dma((4,)), dma((3, LE, 4)), dma((8,)), dma((2,)),
         ],
         compiler_params=pltpu.CompilerParams(
-            collective_id=0, has_side_effects=True, vmem_limit_bytes=48 << 20
+            collective_id=0, has_side_effects=True, vmem_limit_bytes=58 << 20
         ),
         name="dispatch",
-    )(mine, info)
-
-
-def nt(a, b):
-    return lax.dot_general(a, b, (((1,), (1,)), ((), ())), preferred_element_type=F32)
-
-
-def tn(a, b):
-    return lax.dot_general(a, b, (((0,), (0,)), ((), ())), preferred_element_type=F32)
-
-
-def expert_kernel(rows, w_gate, w_up, w_down, g_gate, g_up, g_down, part, probs):
-    def cut(q):
-        return slice(q * LANES, (q + 1) * LANES)
-
-    gate = sum(nt(rows[q, 0], w_gate[0, :, cut(q)]) for q in range(4))
-    up = sum(nt(rows[q, 0], w_up[0, :, cut(q)]) for q in range(4))
-    back = sum(nt(rows[4 + q, 0], w_down[0, :, cut(q)]) for q in range(4))
-    sig = 1.0 / (1.0 + jnp.exp(-gate))
-    act = gate * sig
-    hidden = (act * up).astype(BF)
-    d_gate = (back * up * sig * (1.0 + gate * (1.0 - sig))).astype(BF)
-    d_up = (back * act).astype(BF)
-    product = (hidden.astype(F32) * back).astype(BF)
-    ones = jnp.ones((16, product.shape[1]), BF)
-    probs[...] = jnp.zeros_like(probs)
-    for yy in range(NY):
-        for g in range(2):
-            at = (2 * yy + g) * GROUP
-            probs[0, yy, g, :, 0:GROUP] = nt(ones, product[at : at + GROUP]).astype(BF)
-    for q in range(4):
-        g_down[0, :, cut(q)] = tn(hidden, rows[4 + q, 0]).astype(BF)
-        g_gate[0, :, cut(q)] = tn(d_gate, rows[q, 0]).astype(BF)
-        g_up[0, :, cut(q)] = tn(d_up, rows[q, 0]).astype(BF)
-        sent = (
-            jnp.dot(d_gate, w_gate[0, :, cut(q)], preferred_element_type=F32)
-            + jnp.dot(d_up, w_up[0, :, cut(q)], preferred_element_type=F32)
-        ).astype(BF)
-        part[2 * q, 0] = sent[:, :WIDE]
-        part[2 * q + 1, 0] = sent[:, WIDE:]
-
-
-def experts(rows, w_gate, w_up, w_down):
-    le, hid, width = w_gate.shape
-    n = rows.shape[2]
-    weight = pl.BlockSpec((1, hid, width), lambda i: (i, 0, 0))
-    return pl.pallas_call(
-        expert_kernel,
-        grid=(le,),
-        out_shape=(
-            jax.ShapeDtypeStruct((le, hid, width), BF),
-            jax.ShapeDtypeStruct((le, hid, width), BF),
-            jax.ShapeDtypeStruct((le, hid, width), BF),
-            jax.ShapeDtypeStruct((8, le, n, WIDE), BF),
-            jax.ShapeDtypeStruct((le, NY, 2, 16, TOK), BF),
-        ),
-        in_specs=[pl.BlockSpec((8, 1, n, LANES), lambda i: (0, i, 0, 0)), weight, weight, weight],
-        out_specs=(
-            weight, weight, weight,
-            pl.BlockSpec((8, 1, n, WIDE), lambda i: (0, i, 0, 0)),
-            pl.BlockSpec((1, NY, 2, 16, TOK), lambda i: (i, 0, 0, 0, 0)),
-        ),
-        compiler_params=pltpu.CompilerParams(vmem_limit_bytes=56 << 20),
-        cost_estimate=pl.CostEstimate(flops=8_000_000_000, bytes_accessed=25_000_000, transcendentals=250_000),
-        name="experts",
-    )(rows, w_gate, w_up, w_down)
+    )(mine, info, w_gate, w_up, w_down)
 
 
 def return_kernel(
-    part, probs, goals, info, grads, grad_probs,
-    own, x_in, kept, y_in, relay, pick, pick_t, sums, p_in, z_out, z_in, f_out, f_in, v_out, v_in, b_in, b_all, b_out,
-    o_sem, x_send, x_recv, y_send, y_recv, r_send, r_recv, p_send, p_recv, z_send, z_recv, f_send, f_recv,
-    b_send, b_recv, v_send, v_recv, g_send, g_recv,
+    rows_in, pick_in, pick_t_in, inner, w_gate, w_up, probs, info, grads, grad_probs, g_gate, g_up, g_down,
+    rows, held, turned, made, x_out, x_in, kept, y_in, relay, pick, pick_t, sums, p_in, z_out, z_in, f_out, f_in, v_out, v_in, b_in, b_all, b_out,
+    o_sem, w_sem, m_sem, x_send, x_recv, y_send, y_recv, r_send, r_recv, p_send, p_recv, z_send, z_recv, f_send, f_recv,
+    b_send, b_recv, v_send, v_recv, g_send, g_recv, t_sem,
 ):
     y, z, c, x = axes()
     h = x % 2
@@ -371,6 +384,18 @@
         pl.semaphore_signal(barrier, inc=1, device_id={"y": (y + m) % NY}, device_id_type=MESH)
     for m in range(1, NX):
         pl.semaphore_signal(barrier, inc=1, device_id={"x": (x + m) % NX}, device_id_type=MESH)
+    loads = [
+        pltpu.make_async_copy(w.at[le, :, pl.ds(j * WIDE, WIDE)], held.at[i, le, j], w_sem.at[i, le, j])
+        for i, w in enumerate((w_gate, w_up))
+        for le in range(LE)
+        for j in range(8)
+    ]
+    picks = [
+        pltpu.make_async_copy(pick_in, pick, t_sem.at[0]),
+        pltpu.make_async_copy(pick_t_in, pick_t, t_sem.at[1]),
+    ]
+    for copy in loads + picks:
+        copy.start()
     pl.semaphore_wait(barrier, 2 * NZ - 1 + NY - 1 + NX - 1)
 
     waits = []
@@ -381,46 +406,67 @@
 
     def x_copy(j, le):
         return remote(
-            part.at[4 * (1 - h) + j, le], x_in.at[j, le], x_send.at[j, le], x_recv.at[j, le],
+            x_out.at[j, le], x_in.at[j, le], x_send.at[j, le], x_recv.at[j, le],
             x=x_up if le == 0 else x_down,
         )
 
-    def own_copy(j):
-        return pltpu.make_async_copy(part.at[4 * h + j], own.at[j], o_sem.at[j])
+    def part(j, le):
+        got = jnp.dot(inner[le, 1], held[0, le, j], preferred_element_type=F32)
+        got += jnp.dot(inner[le, 2], held[1, le, j], preferred_element_type=F32)
+        return got.reshape(NY, 2, GROUP, WIDE)
+
+    def fetch(slot):
+        return pltpu.make_async_copy(rows_in.at[slot], rows.at[slot], o_sem.at[slot])
+
+    def turn():
+        hid = inner.shape[3]
+        same = (
+            lax.broadcasted_iota(jnp.int32, (hid, hid), 0) == lax.broadcasted_iota(jnp.int32, (hid, hid), 1)
+        ).astype(F32).astype(BF)
+        for le in range(LE):
+            for i in range(3):
+                turned[le, i] = nt(same, inner[le, i]).astype(BF)
+
+    def grad_copy(i, le, q):
+        out = (g_down, g_gate, g_up)[i]
+        return pltpu.make_async_copy(
+            made.at[i, le, q], out.at[le, :, pl.ds(q * LANES, LANES)], m_sem.at[i, le, q]
+        )
+
+    def weight_stage(le, q):
+        fetch(q).wait() if le == 0 else None
+        fetch(4 + q).wait() if le == 0 else None
+        for i in range(3):
+            some = rows[4 + q if i == 0 else q, le].reshape(NY * 2 * GROUP, LANES)
+            made[i, le, q] = jnp.dot(turned[le, i], some, preferred_element_type=F32).astype(BF)
+            grad_copy(i, le, q).start()
 
     def b_copy(m):
         return remote(
             probs.at[:, (y + NY - m) % NY], b_in.at[m], b_send.at[m], b_recv.at[m], y=(y + NY - m) % NY
         )
 
+    for copy in loads:
+        copy.wait()
     for m in range(1, NY):
         go(b_copy(m))
     for j in range(4):
         for le in range(LE):
+            x_out[j, le] = part(4 * (1 - h) + j, le).astype(BF)
             go(x_copy(j, le))
-        own_copy(j).start()
+    for slot in range(8):
+        fetch(slot).start()
     b_own = pltpu.make_async_copy(probs.at[:, y], b_in.at[0], b_send.at[0])
     b_own.start()
 
-    slot_row = lax.broadcasted_iota(jnp.int32, (GROUP, TOK), 0).astype(F32)
-    same_lane = (
-        lax.broadcasted_iota(jnp.int32, (TOK, TOK), 0) == lax.broadcasted_iota(jnp.int32, (TOK, TOK), 1)
-    ).astype(F32).astype(BF)
-    for s in range(NZ * NC):
-        g, i = s // 8, s % 8
-        goal = goals[s]
-        for e in range(NY * LE):
-            pick[g, pl.ds(e * GROUP, GROUP), pl.ds(i * TOK, TOK)] = jnp.where(
-                slot_row == goal[e : e + 1], 1.0, 0.0
-            ).astype(BF)
-        pick_t[g, pl.ds(i * TOK, TOK), :] = nt(same_lane, pick[g, :, pl.ds(i * TOK, TOK)]).astype(BF)
-
     def v_copy(at, r, cc, far):
         back = PLACE[(NZ - r) % NZ]
         return remote(
             v_out.at[at, cc], v_in.at[back, c], v_send.at[at, far], v_recv.at[back, c], z=(z + r) % NZ, c=cc
         )
 
+    for copy in picks:
+        copy.wait()
     b_own.wait()
     for m in range(1, NY):
         b_copy(m).wait_recv()
@@ -458,10 +504,10 @@
         )
 
     def x_stage(j):
-        own_copy(j).wait()
-        for le in range(LE):
+        for le in range(LE):
+            own = part(4 * h + j, le)
             x_copy(j, le).wait_recv()
-            kept[j, le] = (own[j, le].astype(F32) + x_in[j, le].astype(F32)).astype(BF)
+            kept[j, le] = (own + x_in[j, le].astype(F32)).astype(BF)
             go(y_copy(j, 2, le))
             go(y_copy(j, 1, le))
             go(y_copy(j, 3, le))
@@ -577,6 +623,9 @@
         events += [(2 * j + 3 + (4 - s), j, z_stage, (j, s)) for s in (4, 3, 2, 1)]
         events += [(2 * j + 7, j, home_stage, (j,)), (2 * j + 9, j, end_stage, (j,))]
     events.append((7.5, 0, gate_stage, ()))
+    events.append((0.5, 0, turn, ()))
+    for n in range(8):
+        events.append((2.6 + n, 0, weight_stage, (n // 4, n % 4)))
     for _, _, stage, given in sorted(events, key=lambda e: (e[0], e[1])):
         stage(*given)
     b_all[x] = b_out[...]
@@ -587,11 +636,17 @@
         b_all[0].astype(F32) + b_all[1].astype(F32) + b_all[2].astype(F32) + b_all[3].astype(F32)
     )
     grad_probs[...] = total[:8] / info[...].astype(F32)[8:]
+    for i in range(3):
+        for le in range(LE):
+            for q in range(4):
+                grad_copy(i, le, q).wait()
     for copy in waits:
         copy.wait_send()
 
 
-def give_back(part, probs, goals, info):
+def give_back(rows, pick, pick_t, inner, w_gate, w_up, probs, info):
+    hid = w_gate.shape[1]
+    count = NY * 2 * GROUP
     vmem = pl.BlockSpec(memory_space=pltpu.VMEM)
     anyw = pl.BlockSpec(memory_space=pl.ANY)
     dma = pltpu.SemaphoreType.DMA
@@ -600,10 +655,17 @@
         out_shape=(
             jax.ShapeDtypeStruct((8, TOK, WIDE), BF),
             jax.ShapeDtypeStruct((8, TOK), F32),
+            jax.ShapeDtypeStruct(w_gate.shape, BF),
+            jax.ShapeDtypeStruct(w_gate.shape, BF),
+            jax.ShapeDtypeStruct(w_gate.shape, BF),
         ),
-        in_specs=[anyw, vmem, vmem, vmem],
-        out_specs=(vmem, vmem),
+        in_specs=[anyw, anyw, anyw, vmem, anyw, anyw, vmem, vmem],
+        out_specs=(vmem, vmem, anyw, anyw, anyw),
         scratch_shapes=[
+            pltpu.VMEM((8, LE, NY, 2, GROUP, LANES), BF),
+            pltpu.VMEM((2, LE, 8, hid, WIDE), BF),
+            pltpu.VMEM((LE, 3, hid, count), BF),
+            pltpu.VMEM((3, LE, 4, hid, LANES), BF),
             pltpu.VMEM((4, LE, NY, 2, GROUP, WIDE), BF),
             pltpu.VMEM((4, LE, NY, 2, GROUP, WIDE), BF),
             pltpu.VMEM((4, LE, NY, 2, GROUP, WIDE), BF),
@@ -622,7 +684,7 @@
             pltpu.VMEM((NY, LE, 2, 16, TOK), BF),
             pltpu.VMEM((NX, 16, TOK), BF),
             pltpu.VMEM((16, TOK), BF),
-            dma((4,)),
+            dma((8,)), dma((2, LE, 8)), dma((3, LE, 4)),
             dma((4, LE)), dma((4, LE)),
             dma((4, 3, LE)), dma((4, 3, LE)),
             dma((4, LE)), dma((4, LE)),
@@ -631,13 +693,13 @@
             dma((4, 3)), dma((4, 3)),
             dma((NY,)), dma((NY,)),
             dma((NZ, 2)), dma((NZ, NC)),
-            dma((NX,)), dma((NX,)),
+            dma((NX,)), dma((NX,)), dma((2,)),
         ],
         compiler_params=pltpu.CompilerParams(
-            collective_id=1, has_side_effects=True, vmem_limit_bytes=48 << 20
+            collective_id=1, has_side_effects=True, vmem_limit_bytes=58 << 20
         ),
         name="give_back",
-    )(part, probs, goals, info)
+    )(rows, pick, pick_t, inner, w_gate, w_up, probs, info)
 
 
 def body(tokens, grad_out, routes, probs, w_gate, w_up, w_down):
@@ -650,12 +712,9 @@
         ]
     )
     info = jnp.concatenate([routes.T.astype(BF), probs.T], axis=0)
-    rows, goals = dispatch(mine, info)
-    g_gate, g_up, g_down, part, prob = experts(
-        rows.reshape(8, LE, NY * 2 * GROUP, LANES), w_gate, w_up, w_down
-    )
-    grads, grad_probs = give_back(
-        part.reshape(8, LE, NY, 2, GROUP, WIDE), prob, goals, info
+    rows, pick, pick_t, inner, prob = dispatch(mine, info, w_gate, w_up, w_down)
+    grads, grad_probs, g_gate, g_up, g_down = give_back(
+        rows, pick, pick_t, inner, w_gate, w_up, prob, info
     )
     grad_tokens = jnp.transpose(grads, (1, 0, 2)).reshape(tokens.shape)
     return (grad_tokens, grad_probs.T.astype(BF), g_gate, g_up, g_down)

time: 212 us -> 212 us (level)
  Pallas kernels: 202 us -> 199 us
  local copies, waits for them, and re-layouts: 5.76 us -> 8.67 us
    pallas_call x1 -> x0, Pallas kernels: 19.3 us -> none  [experts(): pl.pallas_call(expert_kernel, grid=(le,), out_shape=(jax.ShapeDtypeStruct...]
    pallas_call x1, Pallas kernels: 104 us -> 114 us  [dispatch(): pl.pallas_call(dispatch_kernel, out_shape=(jax.ShapeDtypeStruct((8, LE, N...]
    pallas_call x1, Pallas kernels: 79.2 us -> 85.5 us  [give_back(): pl.pallas_call(return_kernel, out_shape=(jax.ShapeDtypeStruct((8, TOK, WI...]
    unnamed x5 -> x12, local copies, waits for them, and re-layouts: 4.34 us -> 6.11 us
where the time goes in v2:
time: 212 us
  Pallas kernels  199 us (94%)
  local copies, waits for them, and re-layouts  8.67 us (4%)
  other arithmetic  3.41 us (2%)
    pallas_call x1, Pallas kernels, dispatch(): pl.pallas_call(dispatch_kernel, out_shape=(jax.ShapeDtypeStruct((8, LE, N...  114 us
    pallas_call x1, Pallas kernels, give_back(): pl.pallas_call(return_kernel, out_shape=(jax.ShapeDtypeStruct((8, TOK, WI...  85.5 us
    unnamed x12, local copies, waits for them, and re-layouts  6.11 us

profile of v2, /device:TPU:8, one launch (start us, length us, event | category | flops | bytes accessed | tf_op | source)
XLA Modules:
  0.0 211.8 jit_solution(4991407921540331301)
XLA Ops:
  0.7 0.7 convert_bitcast_fusion.1
  1.3 1.3 pad_maximum_fusion.1.info
  2.6 1.1 dynamic-slice_bitcast_fusion.1
  3.8 0.9 pad_maximum_fusion.mine
  4.6 113.6 %dispatch.1 = (bf16[8,2,4,2,80,512]{5,4,3,2,1,0:T(8,128)(2,1)}, bf16[2,640,1024]{2,1,0:T(8,128)(2,1)}, bf16[2,1024,640]{2,1,0:T(8,128)(2,1)}, bf16[2,3,640,192]{...) custom-call(bf16[4,128,512]{2,1,0:T(8,128)(2,1)} %pad_maximum_fusion.mine, bf16[16,128]{1,0:T(8,128)(2,1)} %pad_maximum_fusion.1.info, ...), custom_call_target="tpu_custom_call" | custom-call | tf_op jit(solution)/shard_map/dispatch/pallas_call | solution.py:327
  118.2 85.5 %give_back.1 = (bf16[8,128,256]{2,1,0:T(8,128)(2,1)}, f32[8,128]{1,0:T(8,128)}, bf16[2,192,2048]{2,1,0:T(8,128)(2,1)}, bf16[2,192,2048]{2,1,0:T(8,128)(2,1)}, bf16[2,192,2048]{2,1,0:T(8,128)(2,1)}) custom-call(bf16[8,2,4,2,80,512]{5,4,3,2,1,0:T(8,128)(2,1)} %get-tuple-element.15.rows_in, bf16[2,640,1024]{2,1,0:T(8,128)(2,1)} %get-tuple-element.16.pick_in, ...), custom_call_target="tpu_custom_call" | custom-call | tf_op jit(solution)/shard_map/give_back/pallas_call | solution.py:653
  203.7 0.0 copy-start.3
  203.7 0.0 copy-start.2
  203.7 1.4 copy.12
  205.1 1.0 copy.13
  206.1 0.0 copy-done.3
  206.1 0.6 convert_bitcast_fusion
  206.7 0.0 copy-done.2
  206.7 0.0 copy-start.1
  206.7 1.1 copy.17
  207.9 0.8 copy-done.1
  208.7 0.0 copy-start
  208.7 1.1 copy.18
  209.8 0.8 copy-done
  210.7 1.1 copy.19
Async XLA Ops:
  203.7 2.5 %copy-start.3 = (f32[8,128]{1,0:T(8,128)S(1)}, f32[8,128]{1,0:T(8,128)}, u32[]{:S(2)}) copy-start(f32[8,128]{1,0:T(8,128)} %get-tuple-element.21) | copy-start | bytes 12292
  203.7 3.0 %copy-start.2 = (bf16[2,192,2048]{2,1,0:T(8,128)(2,1)S(1)}, bf16[2,192,2048]{2,1,0:T(8,128)(2,1)}, u32[]{:S(2)}) copy-start(bf16[2,192,2048]{2,1,0:T(8,128)(2,1)} %get-tuple-element.43) | copy-start | bytes 4718596
  206.7 2.0 copy-start.1
  208.7 2.0 copy-start

commit v3 on v2

--- a/solution.py
+++ b/solution.py
@@ -11,7 +11,8 @@
 TOK = 128
 GROUP = 4 * NC * SLOTS
 LANES = 512
-WIDE = 256
+HALF = 2 * LANES
+CUTS = [pl.ds(0, 384), pl.ds(384, 256), pl.ds(640, 256), pl.ds(896, 128)]
 BF = jnp.bfloat16
 F32 = jnp.float32
 MESH = pl.DeviceIdType.MESH
@@ -34,7 +35,7 @@
 
 def dispatch_kernel(
     mine, info, w_gate, w_up, w_down, rows_out, pick_out, pick_t_out, inner, probs,
-    rows, held, acc, blocks, infos, pick, pick_t, pick_w, out_y, relay,
+    rows, held, acc, blocks, table, infos, pick, pick_t, pick_w, out_y, relay,
     i_send, i_recv, z_send, z_recv, p_send, p_recv, y_send, y_recv, r_send, r_recv, x_send, x_recv, l_sem, w_sem, o_sem, t_sem,
 ):
     y, z, c, x = axes()
@@ -61,6 +62,30 @@
     ]
     for copy in loads:
         copy.start()
+    row = lax.broadcasted_iota(jnp.int32, (NY * LE, TOK), 0)
+    column = (y + row // LE) % NY * (NZ * NC * LE) + row % LE
+    before = (
+        lax.broadcasted_iota(jnp.int32, (TOK, TOK), 0) < lax.broadcasted_iota(jnp.int32, (TOK, TOK), 1)
+    ).astype(F32).astype(BF)
+    named = info[...].astype(F32)
+    hits, weights = [], []
+    for m in range(NZ):
+        for cc in range(NC):
+            expert = (column + ((z + m) % NZ * NC + cc) * LE).astype(F32)
+            hit = jnp.zeros((NY * LE, TOK), F32)
+            weight = jnp.zeros((NY * LE, TOK), F32)
+            for k in range(8):
+                same = named[k : k + 1] == expert
+                hit = jnp.where(same, 1.0, hit)
+                weight = jnp.where(same, named[8 + k : 9 + k], weight)
+            hits.append(hit)
+            weights.append(weight)
+    ranks = jnp.dot(jnp.concatenate(hits, axis=0).astype(BF), before, preferred_element_type=F32)
+    for m in range(NZ):
+        for cc in range(NC):
+            n = m * NC + cc
+            slots = jnp.where(hits[n] > 0, ranks[n * NY * LE : (n + 1) * NY * LE], -1.0)
+            table[m, cc] = jnp.concatenate([slots, weights[n]], axis=0).astype(BF)
     pick[...] = jnp.zeros_like(pick)
     pick_w[...] = jnp.zeros_like(pick_w)
     acc[...] = jnp.zeros_like(acc)
@@ -75,7 +100,7 @@
     def info_copy(m, cc, far):
         at = PLACE[(NZ - m) % NZ]
         return remote(
-            info, infos.at[at, c], i_send.at[m, far], i_recv.at[at, c], z=(z + m) % NZ, c=cc
+            table.at[m, cc], infos.at[at, c], i_send.at[m, far], i_recv.at[at, c], z=(z + m) % NZ, c=cc
         )
 
     for m in range(NZ):
@@ -229,43 +254,26 @@
             relayed(k, g, le).wait_recv()
             go(x_piece(k, g, 2, le))
 
-    infos[0, c] = info[...]
-    for at in range(NZ):
-        if at:
-            remote(info, infos.at[at, c], i_send.at[0, 0], i_recv.at[at, c], c=other).wait_recv()
-        remote(info, infos.at[at, other], i_send.at[0, 0], i_recv.at[at, other], c=other).wait_recv()
-
-    row = lax.broadcasted_iota(jnp.int32, (NY * LE, TOK), 0)
-    expert = ((((y + row // LE) % NY * NZ + z) * NC + c) * LE + row % LE).astype(F32)
-    before = (
-        lax.broadcasted_iota(jnp.int32, (TOK, TOK), 0) < lax.broadcasted_iota(jnp.int32, (TOK, TOK), 1)
-    ).astype(F32).astype(BF)
-    hits, weights = [], []
-    for at in range(NZ):
-        for cc in range(NC):
-            named = infos[at, cc].astype(F32)
-            hit = jnp.zeros((NY * LE, TOK), F32)
-            weight = jnp.zeros((NY * LE, TOK), F32)
-            for k in range(8):
-                same = named[k : k + 1] == expert
-                hit = jnp.where(same, 1.0, hit)
-                weight = jnp.where(same, named[8 + k : 9 + k], weight)
-            hits.append(hit)
-            weights.append(weight)
-    ranks = jnp.dot(jnp.concatenate(hits, axis=0).astype(BF), before, preferred_element_type=F32)
-    slot_row = lax.broadcasted_iota(jnp.int32, (16, TOK), 0).astype(F32)
-    for s in range(NZ * NC):
-        g, i = s // 8, s % 8
-        first, last = SLOTS * i // 16, (SLOTS * i + SLOTS - 1) // 16
-        goal = jnp.where(
-            hits[s] > 0, ranks[s * NY * LE : (s + 1) * NY * LE] + float(SLOTS * i), -1.0
-        )
-        for e in range(NY * LE):
-            for tile in range(first, last + 1):
-                same = slot_row == goal[e : e + 1] - float(16 * tile)
-                at = (g, pl.ds(e * GROUP + 16 * tile, 16), pl.ds(i * TOK, TOK))
-                pick[at] = jnp.where(same, 1.0, 0.0).astype(BF)
-                pick_w[at] = jnp.where(same, weights[s][e : e + 1], 0.0).astype(BF)
+    infos[0, c] = table[0, c]
+
+    def build(g):
+        slot_row = lax.broadcasted_iota(jnp.int32, (16, TOK), 0).astype(F32)
+        for at in range(4 * g, 4 * g + 4):
+            if at:
+                remote(info, infos.at[at, c], i_send.at[0, 0], i_recv.at[at, c], c=other).wait_recv()
+            remote(info, infos.at[at, other], i_send.at[0, 0], i_recv.at[at, other], c=other).wait_recv()
+            for cc in range(NC):
+                i = at % 4 * NC + cc
+                first, last = SLOTS * i // 16, (SLOTS * i + SLOTS - 1) // 16
+                given = infos[at, cc].astype(F32)
+                slots, weight = given[: NY * LE], given[NY * LE :]
+                goal = jnp.where(slots >= 0, slots + float(SLOTS * i), -1.0)
+                for e in range(NY * LE):
+                    for tile in range(first, last + 1):
+                        same = slot_row == goal[e : e + 1] - float(16 * tile)
+                        put = (g, pl.ds(e * GROUP + 16 * tile, 16), pl.ds(i * TOK, TOK))
+                        pick[put] = jnp.where(same, 1.0, 0.0).astype(BF)
+                        pick_w[put] = jnp.where(same, weight[e : e + 1], 0.0).astype(BF)
 
     def pick_copies():
         return [
@@ -295,7 +303,7 @@
         x_landed(k)
         absorb(k, 1 - h)
 
-    events = [(16.0, ready, ()), (16.1, turn, (0,)), (21.0, turn, (1,))]
+    events = [(5.0, build, (0,)), (9.0, build, (1,)), (16.0, ready, ()), (16.1, turn, (0,)), (21.0, turn, (1,))]
     for k in range(4):
         events += [(10 * k + 5 * n - 2, z_step, (k, n)) for n in (1, 2, 3, 4)]
         events += [(10 * k + 8.5, pick_rows, (k, 0)), (10 * k + 18.5, pick_rows, (k, 1))]
@@ -341,6 +349,7 @@
             pltpu.VMEM((LE, 3, count, hid), F32),
             pltpu.VMEM((4, NZ, NC, TOK, LANES), BF),
             pltpu.VMEM((NZ, NC, 16, TOK), BF),
+            pltpu.VMEM((NZ, NC, 16, TOK), BF),
             pltpu.VMEM((2, NY * LE * GROUP, 4 * NC * TOK), BF),
             pltpu.VMEM((2, 4 * NC * TOK, NY * LE * GROUP), BF),
             pltpu.VMEM((2, NY * LE * GROUP, 4 * NC * TOK), BF),
@@ -385,10 +394,10 @@
     for m in range(1, NX):
         pl.semaphore_signal(barrier, inc=1, device_id={"x": (x + m) % NX}, device_id_type=MESH)
     loads = [
-        pltpu.make_async_copy(w.at[le, :, pl.ds(j * WIDE, WIDE)], held.at[i, le, j], w_sem.at[i, le, j])
+        pltpu.make_async_copy(w.at[le, :, pl.ds(j * HALF, HALF)], held.at[i, le, j], w_sem.at[i, le, j])
         for i, w in enumerate((w_gate, w_up))
         for le in range(LE)
-        for j in range(8)
+        for j in range(2)
     ]
     picks = [
         pltpu.make_async_copy(pick_in, pick, t_sem.at[0]),
@@ -406,14 +415,14 @@
 
     def x_copy(j, le):
         return remote(
-            x_out.at[j, le], x_in.at[j, le], x_send.at[j, le], x_recv.at[j, le],
+            x_out.at[le, :, :, :, CUTS[j]], x_in.at[le, :, :, :, CUTS[j]], x_send.at[j, le], x_recv.at[j, le],
             x=x_up if le == 0 else x_down,
         )
 
-    def part(j, le):
-        got = jnp.dot(inner[le, 1], held[0, le, j], preferred_element_type=F32)
-        got += jnp.dot(inner[le, 2], held[1, le, j], preferred_element_type=F32)
-        return got.reshape(NY, 2, GROUP, WIDE)
+    def part(half, j, le):
+        got = jnp.dot(inner[le, 1], held[0, le, half, :, CUTS[j]], preferred_element_type=F32)
+        got += jnp.dot(inner[le, 2], held[1, le, half, :, CUTS[j]], preferred_element_type=F32)
+        return got.reshape(NY, 2, GROUP, CUTS[j].size)
 
     def fetch(slot):
         return pltpu.make_async_copy(rows_in.at[slot], rows.at[slot], o_sem.at[slot])
@@ -452,7 +461,7 @@
         go(b_copy(m))
     for j in range(4):
         for le in range(LE):
-            x_out[j, le] = part(4 * (1 - h) + j, le).astype(BF)
+            x_out[le, :, :, :, CUTS[j]] = part(1 - h, j, le).astype(BF)
             go(x_copy(j, le))
     for slot in range(8):
         fetch(slot).start()
@@ -489,29 +498,29 @@
         go(v_copy(PLACE[r], r, other, 1))
 
     def y_copy(j, d, le):
-        src = kept.at[j, le, (y + NY - d) % NY]
+        src = kept.at[le, (y + NY - d) % NY, :, :, CUTS[j]]
         sems = dict(send=y_send.at[j, d - 1, le], recv=y_recv.at[j, d - 1, le])
         if d == 1:
-            return remote(src, y_in.at[j, :, 1, le], y=y_down, **sems)
+            return remote(src, y_in.at[:, 1, le, :, CUTS[j]], y=y_down, **sems)
         if d == 3:
-            return remote(src, y_in.at[j, :, 3, le], y=y_up, **sems)
-        return remote(src, relay.at[j, le], y=y_up if le == 0 else y_down, **sems)
+            return remote(src, y_in.at[:, 3, le, :, CUTS[j]], y=y_up, **sems)
+        return remote(src, relay.at[le, :, :, CUTS[j]], y=y_up if le == 0 else y_down, **sems)
 
     def relayed(j, le):
         return remote(
-            relay.at[j, le], y_in.at[j, :, 2, le], r_send.at[j, le], r_recv.at[j, le],
+            relay.at[le, :, :, CUTS[j]], y_in.at[:, 2, le, :, CUTS[j]], r_send.at[j, le], r_recv.at[j, le],
             y=y_up if le == 0 else y_down,
         )
 
     def x_stage(j):
         for le in range(LE):
-            own = part(4 * h + j, le)
+            own = part(h, j, le)
             x_copy(j, le).wait_recv()
-            kept[j, le] = (own + x_in[j, le].astype(F32)).astype(BF)
+            kept[le, :, :, :, CUTS[j]] = (own + x_in[le, :, :, :, CUTS[j]].astype(F32)).astype(BF)
             go(y_copy(j, 2, le))
             go(y_copy(j, 1, le))
             go(y_copy(j, 3, le))
-            y_in[j, :, 0, le] = kept[j, le, y]
+            y_in[:, 0, le, :, CUTS[j]] = kept[le, y, :, :, CUTS[j]]
 
     def relay_stage(j):
         for le in range(LE):
@@ -520,7 +529,7 @@
 
     def p_copy(j, g):
         return remote(
-            sums.at[j, g, other], p_in.at[j, g], p_send.at[j, g], p_recv.at[j, g], c=other
+            sums.at[g, other, :, :, CUTS[j]], p_in.at[g, :, :, CUTS[j]], p_send.at[j, g], p_recv.at[j, g], c=other
         )
 
     def sum_stage(j):
@@ -530,10 +539,12 @@
             relayed(j, le).wait_recv()
         for g in (1, 0):
             got = jnp.dot(
-                pick_t[g], y_in[j, g].reshape(NY * LE * GROUP, WIDE), preferred_element_type=F32
-            ).astype(BF).reshape(4, NC, TOK, WIDE)
+                pick_t[g],
+                y_in[g, :, :, :, CUTS[j]].reshape(NY * LE * GROUP, CUTS[j].size),
+                preferred_element_type=F32,
+            ).astype(BF).reshape(4, NC, TOK, CUTS[j].size)
             for cc in range(NC):
-                sums[j, g, cc] = got[:, cc]
+                sums[g, cc, :, :, CUTS[j]] = got[:, cc]
             go(p_copy(j, g))
 
     def place(long, s):
@@ -546,13 +557,13 @@
     def z_copy(j, long, s):
         index = (s - 1) if long else (3 + s)
         return remote(
-            z_out.at[j, index], z_in.at[j, index], z_send.at[j, index], z_recv.at[j, index],
+            z_out.at[index, :, CUTS[j]], z_in.at[index, :, CUTS[j]], z_send.at[j, index], z_recv.at[j, index],
             z=z_short if long else z_long,
         )
 
     def both(j, at):
         g, i = (0, 0) if isinstance(at, int) and at == 0 else (at // 4, at % 4)
-        return sums[j, g, c, i].astype(F32) + p_in[j, g, i].astype(F32)
+        return sums[g, c, i, :, CUTS[j]].astype(F32) + p_in[g, i, :, CUTS[j]].astype(F32)
 
     def z_stage(j, s):
         if s == 4:
@@ -563,29 +574,30 @@
             total = both(j, place(long, s))
             if s < (4 if long else 3):
                 z_copy(j, long, s + 1).wait_recv()
-                total = total + z_in[j, index + 1].astype(F32)
-            z_out[j, index] = total.astype(BF)
+                total = total + z_in[index + 1, :, CUTS[j]].astype(F32)
+            z_out[index, :, CUTS[j]] = total.astype(BF)
             go(z_copy(j, long, s))
 
     def f_copy(j, m):
         return remote(
-            f_out.at[j], f_in.at[j, m - 1], f_send.at[j, m - 1], f_recv.at[j, m - 1], x=(x + m) % NX
+            f_out.at[:, CUTS[j]], f_in.at[m - 1, :, CUTS[j]], f_send.at[j, m - 1], f_recv.at[j, m - 1], x=(x + m) % NX
         )
 
     def home_stage(j):
         total = both(j, 0)
         for long in (True, False):
             z_copy(j, long, 1).wait_recv()
-            total = total + z_in[j, 0 if long else 4].astype(F32)
-        f_out[j] = total.astype(BF)
+            total = total + z_in[0 if long else 4, :, CUTS[j]].astype(F32)
+        f_out[:, CUTS[j]] = total.astype(BF)
         for m in (2, 1, 3):
             go(f_copy(j, m))
 
     def end_stage(j):
         for m in (1, 3, 2):
             f_copy(j, m).wait_recv()
-        grads[4 * (1 - h) + j] = (f_in[j, 0].astype(F32) + f_in[j, 2].astype(F32)).astype(BF)
-        grads[4 * h + j] = (f_out[j].astype(F32) + f_in[j, 1].astype(F32)).astype(BF)
+        cut = CUTS[j]
+        grads[1 - h, :, cut] = (f_in[0, :, cut].astype(F32) + f_in[2, :, cut].astype(F32)).astype(BF)
+        grads[h, :, cut] = (f_out[:, cut].astype(F32) + f_in[1, :, cut].astype(F32)).astype(BF)
 
     def g_copy(m):
         return remote(b_out, b_all.at[x], g_send.at[m], g_recv.at[x], x=(x + m) % NX)
@@ -617,15 +629,19 @@
         for m in range(1, NX):
             go(g_copy(m))
 
-    events = []
-    for j in range(4):
-        events += [(2 * j, j, x_stage, (j,)), (2 * j + 1, j, relay_stage, (j,)), (2 * j + 2, j, sum_stage, (j,))]
-        events += [(2 * j + 3 + (4 - s), j, z_stage, (j, s)) for s in (4, 3, 2, 1)]
-        events += [(2 * j + 7, j, home_stage, (j,)), (2 * j + 9, j, end_stage, (j,))]
-    events.append((7.5, 0, gate_stage, ()))
-    events.append((0.5, 0, turn, ()))
-    for n in range(8):
-        events.append((2.6 + n, 0, weight_stage, (n // 4, n % 4)))
+    events = [(9.0, 0, turn, ()), (33.0, 0, gate_stage, ())]
+    events += [(10.0 + 2 * n, 0, weight_stage, (n // 4, n % 4)) for n in range(8)]
+    for j, cut in enumerate(CUTS):
+        wide = cut.size / 256
+        at = 8 + 32 * (cut.start + cut.size) / HALF
+        events += [(at, j, x_stage, (j,)), (at + 1.5 + 2 * wide, j, relay_stage, (j,))]
+        at += 3 + 7 * wide
+        events.append((at, j, sum_stage, (j,)))
+        at += 1 + 1.5 * wide
+        for n in (4, 3, 2, 1):
+            events.append((at, j, z_stage, (j, n)))
+            at += 1.5 + 1.6 * wide
+        events += [(at, j, home_stage, (j,)), (at + 2 + 3 * wide, j, end_stage, (j,))]
     for _, _, stage, given in sorted(events, key=lambda e: (e[0], e[1])):
         stage(*given)
     b_all[x] = b_out[...]
@@ -653,7 +669,7 @@
     return pl.pallas_call(
         return_kernel,
         out_shape=(
-            jax.ShapeDtypeStruct((8, TOK, WIDE), BF),
+            jax.ShapeDtypeStruct((2, TOK, HALF), BF),
             jax.ShapeDtypeStruct((8, TOK), F32),
             jax.ShapeDtypeStruct(w_gate.shape, BF),
             jax.ShapeDtypeStruct(w_gate.shape, BF),
@@ -663,28 +679,28 @@
         out_specs=(vmem, vmem, anyw, anyw, anyw),
         scratch_shapes=[
             pltpu.VMEM((8, LE, NY, 2, GROUP, LANES), BF),
-            pltpu.VMEM((2, LE, 8, hid, WIDE), BF),
+            pltpu.VMEM((2, LE, 2, hid, HALF), BF),
             pltpu.VMEM((LE, 3, hid, count), BF),
             pltpu.VMEM((3, LE, 4, hid, LANES), BF),
-            pltpu.VMEM((4, LE, NY, 2, GROUP, WIDE), BF),
-            pltpu.VMEM((4, LE, NY, 2, GROUP, WIDE), BF),
-            pltpu.VMEM((4, LE, NY, 2, GROUP, WIDE), BF),
-            pltpu.VMEM((4, 2, NY, LE, GROUP, WIDE), BF),
-            pltpu.VMEM((4, LE, 2, GROUP, WIDE), BF),
+            pltpu.VMEM((LE, NY, 2, GROUP, HALF), BF),
+            pltpu.VMEM((LE, NY, 2, GROUP, HALF), BF),
+            pltpu.VMEM((LE, NY, 2, GROUP, HALF), BF),
+            pltpu.VMEM((2, NY, LE, GROUP, HALF), BF),
+            pltpu.VMEM((LE, 2, GROUP, HALF), BF),
             pltpu.VMEM((2, NY * LE * GROUP, 4 * NC * TOK), BF),
             pltpu.VMEM((2, 4 * NC * TOK, NY * LE * GROUP), BF),
-            pltpu.VMEM((4, 2, NC, 4, TOK, WIDE), BF),
-            pltpu.VMEM((4, 2, 4, TOK, WIDE), BF),
-            pltpu.VMEM((4, 7, TOK, WIDE), BF),
-            pltpu.VMEM((4, 7, TOK, WIDE), BF),
-            pltpu.VMEM((4, TOK, WIDE), BF),
-            pltpu.VMEM((4, 3, TOK, WIDE), BF),
+            pltpu.VMEM((2, NC, 4, TOK, HALF), BF),
+            pltpu.VMEM((2, 4, TOK, HALF), BF),
+            pltpu.VMEM((7, TOK, HALF), BF),
+            pltpu.VMEM((7, TOK, HALF), BF),
+            pltpu.VMEM((TOK, HALF), BF),
+            pltpu.VMEM((3, TOK, HALF), BF),
             pltpu.VMEM((NZ, NC, 16, TOK), BF),
             pltpu.VMEM((NZ, NC, 16, TOK), BF),
             pltpu.VMEM((NY, LE, 2, 16, TOK), BF),
             pltpu.VMEM((NX, 16, TOK), BF),
             pltpu.VMEM((16, TOK), BF),
-            dma((8,)), dma((2, LE, 8)), dma((3, LE, 4)),
+            dma((8,)), dma((2, LE, 2)), dma((3, LE, 4)),
             dma((4, LE)), dma((4, LE)),
             dma((4, 3, LE)), dma((4, 3, LE)),
             dma((4, LE)), dma((4, LE)),

time: 212 us -> 207 us (0.976)
  Pallas kernels: 199 us -> 194 us
    pallas_call x1, Pallas kernels: 85.5 us -> 80.9 us  [give_back(): pl.pallas_call(return_kernel, out_shape=(jax.ShapeDtypeStruct((2, TOK, HA...]
where the time goes in v3:
time: 207 us
  Pallas kernels  194 us (94%)
  local copies, waits for them, and re-layouts  8.67 us (4%)
  other arithmetic  3.41 us (2%)
    pallas_call x1, Pallas kernels, dispatch(): pl.pallas_call(dispatch_kernel, out_shape=(jax.ShapeDtypeStruct((8, LE, N...  113 us
    pallas_call x1, Pallas kernels, give_back(): pl.pallas_call(return_kernel, out_shape=(jax.ShapeDtypeStruct((2, TOK, HA...  80.9 us
    unnamed x12, local copies, waits for them, and re-layouts  6.11 us

profile of v3, /device:TPU:8, one launch (start us, length us, event | category | flops | bytes accessed | tf_op | source)
XLA Modules:
  0.0 207.1 jit_solution(2084235324424544309)
XLA Ops:
  0.7 0.7 convert_bitcast_fusion.1
  1.3 1.3 pad_maximum_fusion.1.info
  2.6 1.1 dynamic-slice_bitcast_fusion.1
  3.8 0.9 pad_maximum_fusion.mine
  4.6 113.4 %dispatch.1 = (bf16[8,2,4,2,80,512]{5,4,3,2,1,0:T(8,128)(2,1)}, bf16[2,640,1024]{2,1,0:T(8,128)(2,1)}, bf16[2,1024,640]{2,1,0:T(8,128)(2,1)}, bf16[2,3,640,192]{...) custom-call(bf16[4,128,512]{2,1,0:T(8,128)(2,1)} %pad_maximum_fusion.mine, bf16[16,128]{1,0:T(8,128)(2,1)} %pad_maximum_fusion.1.info, ...), custom_call_target="tpu_custom_call" | custom-call | tf_op jit(solution)/shard_map/dispatch/pallas_call | solution.py:335
  118.0 80.9 %give_back.1 = (bf16[2,128,1024]{2,1,0:T(8,128)(2,1)}, f32[8,128]{1,0:T(8,128)}, bf16[2,192,2048]{2,1,0:T(8,128)(2,1)}, bf16[2,192,2048]{2,1,0:T(8,128)(2,1)}, bf16[2,192,2048]{2,1,0:T(8,128)(2,1)}) custom-call(bf16[8,2,4,2,80,512]{5,4,3,2,1,0:T(8,128)(2,1)} %get-tuple-element.15.rows_in, bf16[2,640,1024]{2,1,0:T(8,128)(2,1)} %get-tuple-element.16.pick_in, ...), custom_call_target="tpu_custom_call" | custom-call | tf_op jit(solution)/shard_map/give_back/pallas_call | solution.py:669
  198.9 0.0 copy-start.3
  199.0 0.0 copy-start.2
  199.0 1.4 copy.12
  200.4 1.0 copy.13
  201.4 0.0 copy-done.3
  201.4 0.6 convert_bitcast_fusion
  202.0 0.0 copy-done.2
  202.0 0.0 copy-start.1
  202.0 1.1 copy.17
  203.1 0.8 copy-done.1
  204.0 0.0 copy-start
  204.0 1.1 copy.18
  205.1 0.8 copy-done
  205.9 1.1 copy.19
Async XLA Ops:
  198.9 2.5 %copy-start.3 = (f32[8,128]{1,0:T(8,128)S(1)}, f32[8,128]{1,0:T(8,128)}, u32[]{:S(2)}) copy-start(f32[8,128]{1,0:T(8,128)} %get-tuple-element.21) | copy-start | bytes 12292
  199.0 3.0 %copy-start.2 = (bf16[2,192,2048]{2,1,0:T(8,128)(2,1)S(1)}, bf16[2,192,2048]{2,1,0:T(8,128)(2,1)}, u32[]{:S(2)}) copy-start(bf16[2,192,2048]{2,1,0:T(8,128)(2,1)} %get-tuple-element.43) | copy-start | bytes 4718596
  202.0 2.0 copy-start.1
  204.0 2.0 copy-start

commit v4 on v3

--- a/solution.py
+++ b/solution.py
@@ -34,7 +34,7 @@
 
 
 def dispatch_kernel(
-    mine, info, w_gate, w_up, w_down, rows_out, pick_out, pick_t_out, inner, probs,
+    tokens, grad_out, info, w_gate, w_up, w_down, rows_out, pick_out, pick_t_out, inner, probs,
     rows, held, acc, blocks, table, infos, pick, pick_t, pick_w, out_y, relay,
     i_send, i_recv, z_send, z_recv, p_send, p_recv, y_send, y_recv, r_send, r_recv, x_send, x_recv, l_sem, w_sem, o_sem, t_sem,
 ):
@@ -117,21 +117,25 @@
 
     def hop(k, long, s):
         index = (s - 1) if long else (3 + s)
-        src = mine.at[k] if s == 1 else blocks.at[k, place(long, s - 1), c]
+        src = mine(k) if s == 1 else blocks.at[k, place(long, s - 1), c]
         return remote(
             src, blocks.at[k, place(long, s), c], z_send.at[k, index], z_recv.at[k, index],
             z=z_long if long else z_short,
         )
 
     def to_partner(k, at):
-        src = mine.at[k] if isinstance(at, int) and at == 0 else blocks.at[k, at, c]
+        src = mine(k) if isinstance(at, int) and at == 0 else blocks.at[k, at, c]
         return remote(src, blocks.at[k, at, c], p_send.at[k, at], p_recv.at[k, at], c=other)
+
+    def mine(k):
+        at = pl.multiple_of(h * HALF + k % 2 * LANES, LANES)
+        return (tokens if k < 2 else grad_out).at[:, pl.ds(at, LANES)]
 
     def start_chunk(k):
         go(hop(k, True, 1))
         go(hop(k, False, 1))
         go(to_partner(k, 0))
-        keep = pltpu.make_async_copy(mine.at[k], blocks.at[k, 0, c], l_sem.at[k])
+        keep = pltpu.make_async_copy(mine(k), blocks.at[k, 0, c], l_sem.at[k])
         keep.start()
         return keep
 
@@ -220,7 +224,7 @@
             keeps.pop(k).wait()
         for at in range(4 * g, 4 * g + 4):
             remote(
-                mine.at[k], blocks.at[k, at, other], p_send.at[k, at], p_recv.at[k, at], c=other
+                mine(k), blocks.at[k, at, other], p_send.at[k, at], p_recv.at[k, at], c=other
             ).wait_recv()
         chosen = pick[g] if k < 2 else pick_w[g]
         got = jnp.dot(
@@ -303,18 +307,18 @@
         x_landed(k)
         absorb(k, 1 - h)
 
-    events = [(5.0, build, (0,)), (9.0, build, (1,)), (16.0, ready, ()), (16.1, turn, (0,)), (21.0, turn, (1,))]
+    events = [(4.2, build, (0,)), (8.6, build, (1,)), (16.0, ready, ()), (16.1, turn, (0,)), (18.0, turn, (1,))]
     for k in range(4):
-        events += [(10 * k + 5 * n - 2, z_step, (k, n)) for n in (1, 2, 3, 4)]
-        events += [(10 * k + 8.5, pick_rows, (k, 0)), (10 * k + 18.5, pick_rows, (k, 1))]
+        start = 16 * k
+        events += [(start + 4 * n, z_step, (k, n)) for n in (1, 2, 3, 4)]
+        events += [(start + 8.5, pick_rows, (k, 0)), (start + 16.7, pick_rows, (k, 1))]
         if k:
-            events.append((10 * k - 1.9, begin, (k,)))
+            events.append((start - 7.95, begin, (k,)))
         for g in range(2):
-            n = 2 * k + g
-            events += [(15 + 7.5 * n, y_step, (k, g)), (18.2 + 7.5 * n, y_last, (k, g))]
-        end = 18.2 + 7.5 * (2 * k + 1)
-        events += [(end + 0.1, absorb, (k, h)), (end + 6, other_half, (k,))]
-    events.append((18.2 + 7.5 * 3 + 6.1, activate, ()))
+            at = start + 20.5 + 8 * g
+            events += [(at, y_step, (k, g)), (at + 7.9, y_last, (k, g))]
+        events += [(start + 36.5, absorb, (k, h)), (start + 42.4, other_half, (k,))]
+    events.append((58.5, activate, ()))
     for _, stage, given in sorted(events, key=lambda e: e[0]):
         stage(*given)
     finish()
@@ -326,7 +330,7 @@
         copy.wait_send()
 
 
-def dispatch(mine, info, w_gate, w_up, w_down):
+def dispatch(tokens, grad_out, info, w_gate, w_up, w_down):
     hid = w_gate.shape[1]
     count = NY * 2 * GROUP
     vmem = pl.BlockSpec(memory_space=pltpu.VMEM)
@@ -341,7 +345,7 @@
             jax.ShapeDtypeStruct((LE, 3, count, hid), BF),
             jax.ShapeDtypeStruct((LE, NY, 2, 16, TOK), BF),
         ),
-        in_specs=[vmem, vmem, anyw, anyw, anyw],
+        in_specs=[anyw, anyw, vmem, anyw, anyw, anyw],
         out_specs=(anyw, anyw, anyw, vmem, vmem),
         scratch_shapes=[
             pltpu.VMEM((8, LE, NY, 2, GROUP, LANES), BF),
@@ -367,7 +371,7 @@
             collective_id=0, has_side_effects=True, vmem_limit_bytes=58 << 20
         ),
         name="dispatch",
-    )(mine, info, w_gate, w_up, w_down)
+    )(tokens, grad_out, info, w_gate, w_up, w_down)
 
 
 def return_kernel(
@@ -596,8 +600,10 @@
         for m in (1, 3, 2):
             f_copy(j, m).wait_recv()
         cut = CUTS[j]
-        grads[1 - h, :, cut] = (f_in[0, :, cut].astype(F32) + f_in[2, :, cut].astype(F32)).astype(BF)
-        grads[h, :, cut] = (f_out[:, cut].astype(F32) + f_in[1, :, cut].astype(F32)).astype(BF)
+        there = pl.ds(pl.multiple_of((1 - h) * HALF + cut.start, 128), cut.size)
+        here = pl.ds(pl.multiple_of(h * HALF + cut.start, 128), cut.size)
+        grads[:, there] = (f_in[0, :, cut].astype(F32) + f_in[2, :, cut].astype(F32)).astype(BF)
+        grads[:, here] = (f_out[:, cut].astype(F32) + f_in[1, :, cut].astype(F32)).astype(BF)
 
     def g_copy(m):
         return remote(b_out, b_all.at[x], g_send.at[m], g_recv.at[x], x=(x + m) % NX)
@@ -669,7 +675,7 @@
     return pl.pallas_call(
         return_kernel,
         out_shape=(
-            jax.ShapeDtypeStruct((2, TOK, HALF), BF),
+            jax.ShapeDtypeStruct((TOK, 2 * HALF), BF),
             jax.ShapeDtypeStruct((8, TOK), F32),
             jax.ShapeDtypeStruct(w_gate.shape, BF),
             jax.ShapeDtypeStruct(w_gate.shape, BF),
@@ -719,20 +725,13 @@
 
 
 def body(tokens, grad_out, routes, probs, w_gate, w_up, w_down):
-    h = lax.axis_index("x") % 2
-    mine = jnp.stack(
-        [
-            lax.dynamic_slice_in_dim(a, h * 2 * LANES + q * LANES, LANES, axis=1)
-            for a in (tokens, grad_out)
-            for q in range(2)
-        ]
+    info = jnp.concatenate([routes.T.astype(BF), probs.T], axis=0)
+    rows, pick, pick_t, inner, prob = dispatch(
+        tokens, grad_out, info, w_gate, w_up, w_down
     )
-    info = jnp.concatenate([routes.T.astype(BF), probs.T], axis=0)
-    rows, pick, pick_t, inner, prob = dispatch(mine, info, w_gate, w_up, w_down)
-    grads, grad_probs, g_gate, g_up, g_down = give_back(
+    grad_tokens, grad_probs, g_gate, g_up, g_down = give_back(
         rows, pick, pick_t, inner, w_gate, w_up, prob, info
     )
-    grad_tokens = jnp.transpose(grads, (1, 0, 2)).reshape(tokens.shape)
     return (grad_tokens, grad_probs.T.astype(BF), g_gate, g_up, g_down)
 
 

time: 207 us -> 198 us (0.957)
  Pallas kernels: 194 us -> 186 us
    pallas_call x1, Pallas kernels: 113 us -> 105 us  [dispatch(): pl.pallas_call(dispatch_kernel, out_shape=(jax.ShapeDtypeStruct((8, LE, N...]
    unnamed x12 -> x8, local copies, waits for them, and re-layouts: 6.11 us -> 7.85 us
where the time goes in v4:
time: 198 us
  Pallas kernels  186 us (94%)
  local copies, waits for them, and re-layouts  7.85 us (4%)
  other arithmetic  3.22 us (2%)
    pallas_call x1, Pallas kernels, dispatch(): pl.pallas_call(dispatch_kernel, out_shape=(jax.ShapeDtypeStruct((8, LE, N...  105 us
    pallas_call x1, Pallas kernels, give_back(): pl.pallas_call(return_kernel, out_shape=(jax.ShapeDtypeStruct((TOK, 2 * H...  80.9 us
    unnamed x8, local copies, waits for them, and re-layouts  7.85 us

profile of v4, /device:TPU:8, one launch (start us, length us, event | category | flops | bytes accessed | tf_op | source)
XLA Modules:
  0.0 197.9 jit_solution(7945747398684683232)
XLA Ops:
  0.6 0.7 convert_bitcast_fusion.1
  1.3 1.3 pad_maximum_fusion.info
  2.6 105.3 %dispatch.1 = (bf16[8,2,4,2,80,512]{5,4,3,2,1,0:T(8,128)(2,1)}, bf16[2,640,1024]{2,1,0:T(8,128)(2,1)}, bf16[2,1024,640]{2,1,0:T(8,128)(2,1)}, bf16[2,3,640,192]{...) custom-call(bf16[128,2048]{1,0:T(8,128)(2,1)} %tokens.1, bf16[128,2048]{1,0:T(8,128)(2,1)} %grad_out.1, ...), custom_call_target="tpu_custom_call" | custom-call | tf_op jit(solution)/shard_map/dispatch/pallas_call | solution.py:339
  107.9 80.9 %give_back.1 = (bf16[128,2048]{1,0:T(8,128)(2,1)}, f32[8,128]{1,0:T(8,128)}, bf16[2,192,2048]{2,1,0:T(8,128)(2,1)}, bf16[2,192,2048]{2,1,0:T(8,128)(2,1)}, bf16[2,192,2048]{2,1,0:T(8,128)(2,1)}) custom-call(bf16[8,2,4,2,80,512]{5,4,3,2,1,0:T(8,128)(2,1)} %get-tuple-element.15.rows_in, bf16[2,640,1024]{2,1,0:T(8,128)(2,1)} %get-tuple-element.16.pick_in, ...), custom_call_target="tpu_custom_call" | custom-call | tf_op jit(solution)/shard_map/give_back/pallas_call | solution.py:675
  188.8 1.3 convert_bitcast_fusion
  190.1 1.9 copy.16
  191.9 0.0 copy-start.1
  191.9 2.8 %copy.17 = bf16[2,192,2048]{2,1,0:T(8,128)(2,1)} copy(bf16[2,192,2048]{2,1,0:T(8,128)(2,1)} %get-tuple-element.32) | data formatting | bytes 3145728
  194.8 0.0 copy-done.1
  194.8 0.0 copy-start
  194.8 1.1 copy.18
  195.9 0.8 copy-done
  196.8 1.1 copy.19
Async XLA Ops:
  191.9 2.9 %copy-start.1 = (bf16[2,192,2048]{2,1,0:T(8,128)(2,1)S(1)}, bf16[2,192,2048]{2,1,0:T(8,128)(2,1)}, u32[]{:S(2)}) copy-start(bf16[2,192,2048]{2,1,0:T(8,128)(2,1)} %get-tuple-element.33) | copy-start | bytes 4718596
  194.8 2.0 copy-start
